TPU v7x, 256 devices: a whole 4x4x8 slice. The times are simulated.
256 devices in a mesh: depth: 16 (over x, y), tile: 16 (over z, core).
Axes of the slice: x: 4, y: 4, z: 8, core: 2. Of those that a mesh axis runs over, the one named last changes fastest.
Arguments:
- volume: float32 [256, 1024, 2048], P('depth', 'tile'), may hold values from -6 to 6
- entry_depth: int32 [1024, 2048], P('tile'), may hold values from 0 to 127
- light_dir: float32 [3], replicated, may hold values from 0.2 to 1
- transfer: float32 [4, 3], replicated, may hold values from -6 to 6
Outputs:
- frame_rgba: float32 [4, 1024, 2048], P(None, 'tile', 'depth')
All inputs are finite; a program needn't handle non-finite values.
Results may differ from a plain program's by a relative error of at most 0.0003.
Values sent between devices are 32-bit elements; how exact they have to be, the bound alone decides.
No kernel may reach another device: no remote copies, remote signals or barrier semaphores. Data moves between devices by JAX's collectives and lax.ppermute only.
A program may use at most 128 MiB of HBM per device.

v0:
```python
import jax
import jax.numpy as jnp
from jax import lax
from jax.sharding import PartitionSpec as P


def padded_2(cells, sides, width):
    for axis, dim in sides:
        count = lax.axis_size(axis)
        ends = count - 1
        head = lax.slice_in_dim(cells, 0, width, axis=dim)
        tail = lax.slice_in_dim(cells, cells.shape[dim] - width, cells.shape[dim], axis=dim)
        cells = jnp.concatenate(
            [
                lax.ppermute(tail, axis, [(i, (i + 1) % count) for i in range(ends)]),
                cells,
                lax.ppermute(head, axis, [((i + 1) % count, i) for i in range(ends)]),
            ],
            axis=dim,
        )
    return cells


def swapped(value, axis, apart):
    mask = 2**apart
    pairs = [(source, source ^ mask) for source in range(lax.axis_size(axis))]
    return lax.ppermute(value, axis, pairs)


def emission(padded, depth_pos, entry_depth, light_dir, transfer, depth_total):
    centre = padded[1:-1, 1:-1, 1:-1]
    grad_z = (padded[2:, 1:-1, 1:-1] - padded[:-2, 1:-1, 1:-1]) * 0.5
    grad_x = (padded[1:-1, 2:, 1:-1] - padded[1:-1, :-2, 1:-1]) * 0.5
    grad_y = (padded[1:-1, 1:-1, 2:] - padded[1:-1, 1:-1, :-2]) * 0.5
    grad_norm = jnp.sqrt(grad_z * grad_z + grad_x * grad_x + grad_y * grad_y + 1.0)
    light_norm = jnp.sqrt(jnp.sum(light_dir * light_dir))
    facing = jnp.abs(light_dir[0] * grad_z + light_dir[1] * grad_x + light_dir[2] * grad_y)
    shading = 0.3 + 0.7 * facing / (grad_norm * light_norm)
    opacity = (
        4.0
        / depth_total
        * jax.nn.sigmoid(transfer[3, 0] * centre + transfer[3, 1] * grad_norm + transfer[3, 2])
    )
    opacity = jnp.where(depth_pos[:, None, None] >= entry_depth[None], opacity, 0.0)
    colors = jnp.stack(
        [
            shading
            * jax.nn.sigmoid(transfer[k, 0] * centre + transfer[k, 1] * grad_norm + transfer[k, 2])
            for k in range(3)
        ]
    )
    return (opacity, colors)


def composite(opacity, colors):
    logs = jnp.log1p(-opacity)
    transmit = jnp.exp(jnp.cumsum(logs, axis=0) - logs)
    weight = transmit * opacity
    shaded = jnp.sum(weight[None] * colors, axis=1)
    return jnp.concatenate([shaded, jnp.sum(weight, axis=0)[None]], axis=0)


def local(volume, entry_depth, light_dir, transfer):
    slab_cells, tile_rows, columns = volume.shape
    groups = lax.axis_size("depth")
    device_pos = lax.axis_index("depth")
    extended = padded_2(volume, (("depth", 0), ("tile", 1)), 1)
    padded = jnp.pad(extended, ((0, 0), (0, 0), (1, 1)))
    depth_pos = device_pos * slab_cells + jnp.arange(slab_cells, dtype=jnp.int32)
    opacity, colors = emission(
        padded, depth_pos, entry_depth, light_dir, transfer, float(slab_cells * groups)
    )
    brick_rgba = composite(opacity, colors)
    piece_cols = columns // groups
    holding = brick_rgba.reshape(4, tile_rows, groups, piece_cols)
    levels = groups.bit_length() - 1
    for level in range(levels):
        count = holding.shape[2]
        halves = holding.reshape(4, tile_rows, count // 2, 2, piece_cols)
        lower = halves[:, :, :, 0]
        upper = halves[:, :, :, 1]
        is_front = device_pos // (1 << level) % 2 == 0
        kept_half = jnp.where(is_front, lower, upper)
        given = jnp.where(is_front, upper, lower)
        received = swapped(given, "depth", level)
        front_part = jnp.where(is_front, kept_half, received)
        back_part = jnp.where(is_front, received, kept_half)
        holding = front_part + (1.0 - front_part[3:4]) * back_part
    return holding.reshape(4, tile_rows, piece_cols)


def solution(mesh):
    placed = (P("depth", "tile", None), P("tile", None), P(), P())
    return jax.shard_map(
        local, mesh=mesh, in_specs=placed, out_specs=P(None, "tile", "depth"), check_vma=False
    )
```

profile of v0, /device:TPU:96, one launch (start us, length us, event | category | flops | bytes accessed | tf_op | source)
XLA Modules:
  0.0 195.4 jit_solution(11953855942869394352)
XLA Ops:
  0.0 1.3 fusion.26
  1.3 3.5 %collective-permute-start.1 = (f32[1,64,2048]{2,1,0:T(8,128)S(1)}, f32[1,64,2048]{2,1,0:T(8,128)S(1)}, u32[]{:S(2)}, u32[]{:S(2)}) collective-permute-start(f32[1,64,2048]{2,1,0:T(8,128)S(1)} %get-tuple-element.13), channel_id=1, source_target_pairs={{0,16},{16,32},{32,48},{48,64},{64,80},{80,96},{96,112},{112,128},... | collective-permute-start | bytes 1572872 | tf_op jit(solution)/shard_map/ppermute | solution.py:15
  4.8 1.3 collective-permute-start
  6.1 1.3 multiply_reduce_fusion
  7.4 1.4 fusion.29
  8.8 7.1 %collective-permute-done.1 = f32[1,64,2048]{2,1,0:T(8,128)S(1)} collective-permute-done((f32[1,64,2048]{2,1,0:T(8,128)S(1)}, f32[1,64,2048]{2,1,0:T(8,128)S(1)}, u32[]{:S(2)}, u32[]{:S(2)}) %collective-permute-start.1) | collective-permute-done | bytes 524320 | tf_op jit(solution)/shard_map/ppermute | solution.py:15
  16.0 4.0 %constant_dynamic-update-slice_fusion.1 = f32[18,64,2048]{2,1,0:T(8,128)S(1)} fusion(f32[18,64,2048]{2,1,0:T(8,128)S(1)} %constant_dynamic-update-slice_fusion.2, f32[16,64,2048]{2,1,0:T(8,128)} %param.4), kind=kLoop, calls=%fused_computation.61 | loop fusion | bytes 16777216
  20.1 3.6 %copy-done = f32[18,64,2048]{2,1,0:T(8,128)} copy-done((f32[18,64,2048]{2,1,0:T(8,128)}, f32[18,64,2048]{2,1,0:T(8,128)S(1)}, u32[]{:S(2)}) %copy-start) | copy-done | bytes 9437208
  23.7 0.2 fusion.25
  23.9 1.9 collective-permute-start.2
  25.8 2.4 %collective-permute-start.3 = (f32[18,1,2048]{2,1,0:T(1,128)S(1)}, f32[18,1,2048]{2,1,0:T(1,128)S(1)}, u32[]{:S(2)}, u32[]{:S(2)}) collective-permute-start(f32[18,1,2048]{2,1,0:T(1,128)S(1)} %get-tuple-element.10), channel_id=1, source_target_pairs={{0,1},{1,2},{2,3},{3,4},{4,5},{5,6},{6,7},{7,8},{8,9},{9,10},{10,1... | collective-permute-start | bytes 442376 | tf_op jit(solution)/shard_map/ppermute | solution.py:15
  30.9 0.7 fusion.28
  31.6 0.7 collective-permute-done.3
  32.3 12.2 %select_maximum_fusion = f32[18,66,2050]{2,1,0:T(8,128)} fusion(f32[18,1,2048]{2,1,0:T(1,128)S(1)} %collective-permute-done.2, f32[18,64,2048]{2,1,0:T(8,128)} %copy-done, f32[18,1,2048]{2,1,0:T(1,128)S(1)} %collective-permute-done.3), kind=kLoop, calls=%fused_computation.4 | loop fusion | flops 19483200 | bytes 19473696 | tf_op jit(solution)/shard_map/concatenate | solution.py:13
  44.5 32.0 %multiply_bitcast_fusion.2 = (f32[1,16,64,2048]{3,2,1,0:T(8,128)}, f32[16,64,2048]{2,1,0:T(8,128)}, f32[16,64,2048]{2,1,0:T(8,128)}) fusion(f32[16,64,2048]{2,1,0:T(8,128)S(1)} %bitcast.128, f32[]{:T(128)} %bitcast.8, f32[]{:T(128)} %bitcast.7, f32[]{:T(128)} %bitcast.6, f32[]{:T(128)S(6)} %sqrt.7, f32[]{:T(128)} %bitcast.5, ...), kind=kLoop, calls=%fused_computation.16 | loop fusion | flops 71303168 | bytes 61112348 | tf_op jit(solution)/shard_map/stack | solution.py:45
  76.5 20.1 %fusion.30 = (f32[64,2048]{1,0:T(8,128)}, f32[16,64,2048]{2,1,0:T(8,128)}) fusion(f32[]{:T(128)} %bitcast.2, f32[16,64,2048]{2,1,0:T(8,128)} %get-tuple-element.7, f32[]{:T(128)} %bitcast.1, f32[16,64,2048]{2,1,0:T(8,128)S(1)} %bitcast.128, f32[]{:T(128)} %bitcast, s32[64,2048]{1,0:T(8,128)S(1)} %copy-done.1, s32[16]{0:T(128)S(1)} %iota_add_fusion), kind=kOutput, calls=%fused_computation.75 | output fusion | flops 83755008 | bytes 26214476 | tf_op jit(solution)/shard_map/jit(cumsum)/reduce_window_sum | solution.py:57
  96.6 15.6 %multiply_bitcast_fusion.1 = (f32[1,16,64,2048]{3,2,1,0:T(8,128)}, f32[1,16,64,2048]{3,2,1,0:T(8,128)}) fusion(f32[16,64,2048]{2,1,0:T(8,128)} %get-tuple-element.6, f32[16,64,2048]{2,1,0:T(8,128)} %get-tuple-element.7, f32[16,64,2048]{2,1,0:T(8,128)S(1)} %bitcast.128, f32[]{:T(128)} %bitcast.12, f32[]{:T(128)} %bitcast.11, f32[]{:T(128)} %bitcast.10, ...), kind=kLoop, calls=%fused_computation.15 | loop fusion | flops 33554432 | bytes 41943064 | tf_op jit(solution)/shard_map/stack | solution.py:45
  112.2 12.1 %fusion = f32[3,64,2048]{2,1,0:T(8,128)S(1)} fusion(f32[1,16,64,2048]{3,2,1,0:T(8,128)} %get-tuple-element.9, f32[1,16,64,2048]{3,2,1,0:T(8,128)} %get-tuple-element.8, f32[1,16,64,2048]{3,2,1,0:T(8,128)} %get-tuple-element.5, f32[16,64,2048]{2,1,0:T(8,128)} %get-tuple-element.33), kind=kLoop, calls=%fused_computation.1 | loop fusion | flops 24772608 | bytes 35127296 | tf_op jit(solution)/shard_map/reduce_sum | solution.py:59
  124.3 1.3 concatenate.32
  125.7 1.7 constant_dynamic-update-slice_fusion.4
  127.4 1.5 concatenate.33
  128.8 0.8 constant_dynamic-update-slice_fusion.3
  129.7 5.1 %fusion.27 = (f32[4,64,8,1,128]{4,3,2,1,0:T(1,128)S(1)}, f32[4,64,8,1,128]{4,3,2,1,0:T(1,128)}, f32[4,64,8,1,128]{4,3,2,1,0:T(1,128)S(1)}) fusion(f32[4,64,8,2,128]{4,3,2,1,0:T(2,128)} %constant_dynamic-update-slice_fusion.3, pred[]{:T(512)S(6)} %eq.20), kind=kLoop, calls=%fused_computation.72 | loop fusion | flops 262144 | bytes 5242881 | tf_op jit(solution)/shard_map/slice | solution.py:81
  134.8 2.4 %collective-permute-start.4 = (f32[4,64,8,128]{3,2,1,0:T(8,128)}, f32[4,64,8,128]{3,2,1,0:T(8,128)S(1)}, u32[]{:S(2)}, u32[]{:S(2)}) collective-permute-start(f32[4,64,8,128]{3,2,1,0:T(8,128)} %bitcast.21), channel_id=1, source_target_pairs={{0,16},{16,0},{32,48},{48,32},{64,80},{80,64},{96,112},{112,96},{1... | collective-permute-start | bytes 3145736 | tf_op jit(solution)/shard_map/ppermute | solution.py:27
  137.2 23.1 %collective-permute-done.4 = f32[4,64,8,128]{3,2,1,0:T(8,128)S(1)} collective-permute-done((f32[4,64,8,128]{3,2,1,0:T(8,128)}, f32[4,64,8,128]{3,2,1,0:T(8,128)S(1)}, u32[]{:S(2)}, u32[]{:S(2)}) %collective-permute-start.4) | collective-permute-done | bytes 1048608 | tf_op jit(solution)/shard_map/ppermute | solution.py:27
  160.9 3.8 %collective-permute-start.5 = (f32[4,64,4,128]{3,1,2,0:T(8,128)S(1)}, f32[4,64,4,128]{3,1,2,0:T(8,128)S(1)}, u32[]{:S(2)}, u32[]{:S(2)}) collective-permute-start(f32[4,64,4,128]{3,1,2,0:T(8,128)S(1)} %select_bitcast_fusion), channel_id=1, source_target_pairs={{0,32},{16,48},{32,0},{48,16},{64,96},{80,112},{96,64},{112,80},{1... | collective-permute-start | bytes 1572872 | tf_op jit(solution)/shard_map/ppermute | solution.py:27
  164.8 12.5 %collective-permute-done.5 = f32[4,64,4,128]{3,1,2,0:T(8,128)S(1)} collective-permute-done((f32[4,64,4,128]{3,1,2,0:T(8,128)S(1)}, f32[4,64,4,128]{3,1,2,0:T(8,128)S(1)}, u32[]{:S(2)}, u32[]{:S(2)}) %collective-permute-start.5) | collective-permute-done | bytes 524320 | tf_op jit(solution)/shard_map/ppermute | solution.py:27
  177.6 4.1 %collective-permute-start.6 = (f32[4,64,2,128]{3,1,2,0:T(8,128)S(1)}, f32[4,64,2,128]{3,1,2,0:T(8,128)S(1)}, u32[]{:S(2)}, u32[]{:S(2)}) collective-permute-start(f32[4,64,2,128]{3,1,2,0:T(8,128)S(1)} %select_bitcast_fusion.1), channel_id=1, source_target_pairs={{0,64},{16,80},{32,96},{48,112},{64,0},{80,16},{96,32},{112,48},{1... | collective-permute-start | bytes 786440 | tf_op jit(solution)/shard_map/ppermute | solution.py:27
  181.7 6.3 %collective-permute-done.6 = f32[4,64,2,128]{3,1,2,0:T(8,128)S(1)} collective-permute-done((f32[4,64,2,128]{3,1,2,0:T(8,128)S(1)}, f32[4,64,2,128]{3,1,2,0:T(8,128)S(1)}, u32[]{:S(2)}, u32[]{:S(2)}) %collective-permute-start.6) | collective-permute-done | bytes 262176 | tf_op jit(solution)/shard_map/ppermute | solution.py:27
  188.1 3.4 %collective-permute-start.7 = (f32[4,64,1,128]{3,1,0,2:T(8,128)S(1)}, f32[4,64,1,128]{3,1,0,2:T(8,128)S(1)}, u32[]{:S(2)}, u32[]{:S(2)}) collective-permute-start(f32[4,64,1,128]{3,1,0,2:T(8,128)S(1)} %select_bitcast_fusion.2), channel_id=1, source_target_pairs={{0,128},{16,144},{32,160},{48,176},{64,192},{80,208},{96,224},{112... | collective-permute-start | bytes 393224 | tf_op jit(solution)/shard_map/ppermute | solution.py:27
  191.5 3.2 %collective-permute-done.7 = f32[4,64,1,128]{3,1,0,2:T(8,128)S(1)} collective-permute-done((f32[4,64,1,128]{3,1,0,2:T(8,128)S(1)}, f32[4,64,1,128]{3,1,0,2:T(8,128)S(1)}, u32[]{:S(2)}, u32[]{:S(2)}) %collective-permute-start.7) | collective-permute-done | bytes 131104 | tf_op jit(solution)/shard_map/ppermute | solution.py:27
  194.7 0.7 add_bitcast_fusion.1
  (30 shorter events, 1.3 us)
Async XLA Ops:
  1.3 14.7 %collective-permute-start.1 = (f32[1,64,2048]{2,1,0:T(8,128)S(1)}, f32[1,64,2048]{2,1,0:T(8,128)S(1)}, u32[]{:S(2)}, u32[]{:S(2)}) collective-permute-start(f32[1,64,2048]{2,1,0:T(8,128)S(1)} %get-tuple-element.13), channel_id=1, source_target_pairs={{0,16},{16,32},{32,48},{48,64},{64,80},{80,96},{96,112},{112,128},... | collective-permute-start | bytes 1572872 | tf_op jit(solution)/shard_map/ppermute | solution.py:15
  4.8 15.3 %collective-permute-start = (f32[1,64,2048]{2,1,0:T(8,128)S(1)}, f32[1,64,2048]{2,1,0:T(8,128)S(1)}, u32[]{:S(2)}, u32[]{:S(2)}) collective-permute-start(f32[1,64,2048]{2,1,0:T(8,128)S(1)} %get-tuple-element.12), channel_id=1, source_target_pairs={{16,0},{32,16},{48,32},{64,48},{80,64},{96,80},{112,96},{128,112},... | collective-permute-start | bytes 1572872 | tf_op jit(solution)/shard_map/ppermute | solution.py:17
  16.0 14.9 %copy-start.2 = (f32[4,3]{1,0:T(4,128)S(1)}, f32[4,3]{1,0:T(4,128)}, u32[]{:S(2)}) copy-start(f32[4,3]{1,0:T(4,128)} %param.7) | copy-start | bytes 148
  20.1 3.6 %copy-start = (f32[18,64,2048]{2,1,0:T(8,128)}, f32[18,64,2048]{2,1,0:T(8,128)S(1)}, u32[]{:S(2)}) copy-start(f32[18,64,2048]{2,1,0:T(8,128)S(1)} %constant_dynamic-update-slice_fusion) | copy-start | bytes 28311556
  23.9 7.7 %collective-permute-start.2 = (f32[18,1,2048]{2,1,0:T(1,128)S(1)}, f32[18,1,2048]{2,1,0:T(1,128)S(1)}, u32[]{:S(2)}, u32[]{:S(2)}) collective-permute-start(f32[18,1,2048]{2,1,0:T(1,128)S(1)} %get-tuple-element.11), channel_id=1, source_target_pairs={{1,0},{2,1},{3,2},{4,3},{5,4},{6,5},{7,6},{8,7},{9,8},{10,9},{11,1... | collective-permute-start | bytes 442376 | tf_op jit(solution)/shard_map/ppermute | solution.py:17
  25.8 6.5 %collective-permute-start.3 = (f32[18,1,2048]{2,1,0:T(1,128)S(1)}, f32[18,1,2048]{2,1,0:T(1,128)S(1)}, u32[]{:S(2)}, u32[]{:S(2)}) collective-permute-start(f32[18,1,2048]{2,1,0:T(1,128)S(1)} %get-tuple-element.10), channel_id=1, source_target_pairs={{0,1},{1,2},{2,3},{3,4},{4,5},{5,6},{6,7},{7,8},{8,9},{9,10},{10,1... | collective-permute-start | bytes 442376 | tf_op jit(solution)/shard_map/ppermute | solution.py:15
  30.9 13.6 %slice-start = ((s8[8388608]{0:T(1024)(128)(4,1)}), s8[4194304]{0:T(1024)(128)(4,1)S(1)}, s32[]{:S(2)}) async-start(s8[8388608]{0:T(1024)(128)(4,1)} %bitcast.127), calls=%async_computation | async-start | bytes 8388608
  31.6 12.9 %slice-start.1 = ((s8[8388608]{0:T(1024)(128)(4,1)}), s8[4194304]{0:T(1024)(128)(4,1)S(1)}, s32[]{:S(2)}) async-start(s8[8388608]{0:T(1024)(128)(4,1)} %bitcast.127), calls=%async_computation.1 | async-start | bytes 8388608
  44.5 32.0 %copy-start.1 = (s32[64,2048]{1,0:T(8,128)S(1)}, s32[64,2048]{1,0:T(8,128)}, u32[]{:S(2)}) copy-start(s32[64,2048]{1,0:T(8,128)} %param.5) | copy-start | bytes 1572868
  134.8 25.5 %collective-permute-start.4 = (f32[4,64,8,128]{3,2,1,0:T(8,128)}, f32[4,64,8,128]{3,2,1,0:T(8,128)S(1)}, u32[]{:S(2)}, u32[]{:S(2)}) collective-permute-start(f32[4,64,8,128]{3,2,1,0:T(8,128)} %bitcast.21), channel_id=1, source_target_pairs={{0,16},{16,0},{32,48},{48,32},{64,80},{80,64},{96,112},{112,96},{1... | collective-permute-start | bytes 3145736 | tf_op jit(solution)/shard_map/ppermute | solution.py:27
  160.9 16.4 %collective-permute-start.5 = (f32[4,64,4,128]{3,1,2,0:T(8,128)S(1)}, f32[4,64,4,128]{3,1,2,0:T(8,128)S(1)}, u32[]{:S(2)}, u32[]{:S(2)}) collective-permute-start(f32[4,64,4,128]{3,1,2,0:T(8,128)S(1)} %select_bitcast_fusion), channel_id=1, source_target_pairs={{0,32},{16,48},{32,0},{48,16},{64,96},{80,112},{96,64},{112,80},{1... | collective-permute-start | bytes 1572872 | tf_op jit(solution)/shard_map/ppermute | solution.py:27
  177.6 10.4 %collective-permute-start.6 = (f32[4,64,2,128]{3,1,2,0:T(8,128)S(1)}, f32[4,64,2,128]{3,1,2,0:T(8,128)S(1)}, u32[]{:S(2)}, u32[]{:S(2)}) collective-permute-start(f32[4,64,2,128]{3,1,2,0:T(8,128)S(1)} %select_bitcast_fusion.1), channel_id=1, source_target_pairs={{0,64},{16,80},{32,96},{48,112},{64,0},{80,16},{96,32},{112,48},{1... | collective-permute-start | bytes 786440 | tf_op jit(solution)/shard_map/ppermute | solution.py:27
  188.1 6.6 %collective-permute-start.7 = (f32[4,64,1,128]{3,1,0,2:T(8,128)S(1)}, f32[4,64,1,128]{3,1,0,2:T(8,128)S(1)}, u32[]{:S(2)}, u32[]{:S(2)}) collective-permute-start(f32[4,64,1,128]{3,1,0,2:T(8,128)S(1)} %select_bitcast_fusion.2), channel_id=1, source_target_pairs={{0,128},{16,144},{32,160},{48,176},{64,192},{80,208},{96,224},{112... | collective-permute-start | bytes 393224 | tf_op jit(solution)/shard_map/ppermute | solution.py:27
where the time goes:
time: 196 us; the launch traced here: 195 us
  other arithmetic  99.9 us (51%)
  waiting for transfers between devices  53 us (27%)
  starting transfers between devices  22.8 us (12%)
  local copies, waits for them, and re-layouts  16.8 us (9%)
  between operations  2.87 us (1%)
    another operation x2, other arithmetic, emission(): jnp.stack([shading * jax.nn.sigmoid(transfer[k, 0] * centre + transfer[k,...  47.5 us
    ppermute x4, waiting for transfers between devices, swapped(): return lax.ppermute(value, axis, pairs)  45.1 us
    another operation x1, other arithmetic, composite(): transmit = jnp.exp(jnp.cumsum(logs, axis=0) - logs)  20.1 us
    ppermute x4, starting transfers between devices, swapped(): return lax.ppermute(value, axis, pairs)  13.7 us
    concatenate x1, other arithmetic, padded_2(): jnp.concatenate([lax.ppermute(tail, axis, [(i, (i + 1) % count) for i in...  12.2 us
    reduce_sum x1, other arithmetic, composite(): shaded = jnp.sum(weight[None] * colors, axis=1)  12.1 us
    unnamed x13, local copies, waits for them, and re-layouts  9.29 us
    ppermute x2, waiting for transfers between devices, padded_2(): lax.ppermute(tail, axis, [(i, (i + 1) % count) for i in range(ends)])  7.81 us
  transfers between devices with their start and end apart: 8, of which 7 were waited for; matrix products, arithmetic and copies ran while one was open for 4% of the time, Pallas kernels for 0%

commit v1 on v0

v1 whole, which is shorter than its diff:
```python
import functools

import jax
import jax.numpy as jnp
from jax import lax
from jax.experimental import pallas as pl
from jax.experimental.pallas import tpu as pltpu
from jax.sharding import PartitionSpec as P

ROW = 8
LANE = 128
LOG2E = 1.4426950408889634


def cast_kernel(depth_total, light, transfer, base, volume, front, back, above, below, entry, out, cells, sems):
    step = pl.program_id(0)
    slabs, rows, columns = volume.shape
    tiles = rows // ROW

    def fetch(tile):
        at = pl.ds(pl.multiple_of(tile * ROW, ROW), ROW)
        to = pl.ds(pl.multiple_of(tile * ROW + ROW, ROW), ROW)
        cols = pl.ds(LANE, columns)
        return (
            pltpu.make_async_copy(volume.at[:, at, :], cells.at[pl.ds(1, slabs), to, cols], sems.at[0, tile]),
            pltpu.make_async_copy(front.at[at, :], cells.at[0, to, cols], sems.at[1, tile]),
            pltpu.make_async_copy(back.at[at, :], cells.at[slabs + 1, to, cols], sems.at[2, tile]),
        )

    def fringe():
        cols = pl.ds(LANE, columns)
        inner = pl.ds(1, slabs)
        return (
            pltpu.make_async_copy(above, cells.at[inner, pl.ds(ROW - 1, 1), cols], sems.at[0, tiles]),
            pltpu.make_async_copy(below, cells.at[inner, pl.ds(ROW + rows, 1), cols], sems.at[1, tiles]),
        )

    @pl.when(step == 0)
    def _():
        for copy in fringe():
            copy.start()
        for tile in range(tiles):
            for copy in fetch(tile):
                copy.start()
        blank = jnp.zeros((rows, LANE), jnp.float32)
        for slab in range(1, slabs + 1):
            cells[slab, ROW : ROW + rows, 0:LANE] = blank
            cells[slab, ROW : ROW + rows, LANE + columns : 2 * LANE + columns] = blank
        for copy in fringe():
            copy.wait()
        for copy in fetch(0):
            copy.wait()

    @pl.when(step < tiles - 1)
    def _():
        for copy in fetch(step + 1):
            copy.wait()

    shape = (ROW, LANE)
    lanes = lax.broadcasted_iota(jnp.int32, shape, 1)
    subs = lax.broadcasted_iota(jnp.int32, shape, 0)
    first_lane, last_lane = lanes == 0, lanes == LANE - 1
    first_sub, last_sub = subs == 0, subs == ROW - 1

    def splat(value):
        return jnp.full(shape, value, jnp.float32)

    l0, l1, l2 = (splat(light[i]) for i in range(3))
    scale = 0.35 * lax.rsqrt(l0 * l0 + l1 * l1 + l2 * l2)
    l0, l1, l2 = l0 * scale, l1 * scale, l2 * scale
    hue = [
        (splat(transfer[k, 0] * 0.5), splat(transfer[k, 1] * 0.25), splat(transfer[k, 2] * 0.5))
        for k in range(3)
    ]
    width = jnp.log2(jnp.float32(depth_total / 4.0))
    veil = (
        splat(transfer[3, 0] * -LOG2E),
        splat(transfer[3, 1] * (-0.5 * LOG2E)),
        splat(transfer[3, 2] * -LOG2E + width),
    )
    row_at = pl.ds(pl.multiple_of(step * ROW + ROW, ROW), ROW)
    row_up = pl.ds(pl.multiple_of(step * ROW, ROW), ROW)
    row_dn = pl.ds(pl.multiple_of(step * ROW + 2 * ROW, ROW), ROW)
    origin = base[0]

    def column(k, carry):
        col = pl.ds(pl.multiple_of(k * LANE + LANE, LANE), LANE)
        col_lf = pl.ds(pl.multiple_of(k * LANE, LANE), LANE)
        col_rt = pl.ds(pl.multiple_of(k * LANE + 2 * LANE, LANE), LANE)
        start = entry[:, pl.ds(pl.multiple_of(k * LANE, LANE), LANE)] - origin
        alpha = jnp.zeros(shape, jnp.float32)
        plain = jnp.zeros(shape, jnp.float32)
        tinted = [jnp.zeros(shape, jnp.float32) for _ in range(3)]
        before = cells[0, row_at, col]
        here = cells[1, row_at, col]
        for slab in range(slabs):
            after = cells[slab + 2, row_at, col]
            up = pltpu.roll(jnp.where(last_sub, cells[slab + 1, row_up, col], here), 1, 0)
            dn = pltpu.roll(jnp.where(first_sub, cells[slab + 1, row_dn, col], here), ROW - 1, 0)
            lf = pltpu.roll(jnp.where(last_lane, cells[slab + 1, row_at, col_lf], here), 1, 1)
            rt = pltpu.roll(jnp.where(first_lane, cells[slab + 1, row_at, col_rt], here), LANE - 1, 1)
            gz, gx, gy = after - before, dn - up, rt - lf
            square = gz * gz + gx * gx + gy * gy + 4.0
            inverse = lax.rsqrt(square)
            norm = square * inverse
            shade = 0.15 + jnp.abs(l0 * gz + l1 * gx + l2 * gy) * inverse
            dim = jnp.exp2(veil[0] * here + veil[1] * norm + veil[2])
            root = lax.rsqrt(dim + depth_total / 4.0)
            opacity = jnp.where(start <= slab, root * root, 0.0)
            weight = (1.0 - alpha) * opacity
            alpha = alpha + weight
            lit = weight * shade
            plain = plain + lit
            for c in range(3):
                a, b, o = hue[c]
                tinted[c] = tinted[c] + lit * jnp.tanh(a * here + b * norm + o)
            before, here = here, after
        for c in range(3):
            out[k, c] = plain + tinted[c]
        out[k, 3] = alpha
        return carry

    lax.fori_loop(0, columns // LANE, column, 0)


def cast(volume, front, back, above, below, entry, light, transfer, base, depth_total):
    slabs, rows, columns = volume.shape
    pieces = columns // LANE
    smem = pl.BlockSpec(memory_space=pltpu.SMEM)
    hbm = pl.BlockSpec(memory_space=pl.ANY)
    return pl.pallas_call(
        functools.partial(cast_kernel, depth_total),
        grid=(rows // ROW,),
        in_specs=[smem, smem, smem, hbm, hbm, hbm, hbm, hbm, pl.BlockSpec((ROW, columns), lambda i: (i, 0))],
        out_specs=pl.BlockSpec((pieces, 4, ROW, LANE), lambda i: (0, 0, i, 0)),
        out_shape=jax.ShapeDtypeStruct((pieces, 4, rows, LANE), jnp.float32),
        scratch_shapes=[
            pltpu.VMEM((slabs + 2, rows + 2 * ROW, columns + 2 * LANE), jnp.float32),
            pltpu.SemaphoreType.DMA((3, rows // ROW + 1)),
        ],
        compiler_params=pltpu.CompilerParams(dimension_semantics=("arbitrary",), vmem_limit_bytes=40 * 2**20),
        cost_estimate=pl.CostEstimate(flops=slabs * rows * columns * 60, bytes_accessed=slabs * rows * columns * 5, transcendentals=slabs * rows * columns * 6),
        name="cast",
    )(light, transfer, base, volume, front, back, above, below, entry)


def merge_kernel(parts, out):
    count = parts.shape[0]
    clear = 1.0 - parts[0, 3]
    total = [parts[0, c] for c in range(4)]
    for d in range(1, count):
        total = [total[c] + clear * parts[d, c] for c in range(4)]
        clear = clear * (1.0 - parts[d, 3])
    for c in range(4):
        out[c] = total[c]


def merge(parts):
    count, channels, rows, cols = parts.shape
    return pl.pallas_call(
        merge_kernel,
        grid=(rows // ROW,),
        in_specs=[pl.BlockSpec((count, channels, ROW, cols), lambda i: (0, 0, i, 0))],
        out_specs=pl.BlockSpec((channels, ROW, cols), lambda i: (0, i, 0)),
        out_shape=jax.ShapeDtypeStruct((channels, rows, cols), jnp.float32),
        name="merge",
    )(parts)


def local(volume, entry_depth, light_dir, transfer):
    slabs, rows, columns = volume.shape
    groups = lax.axis_size("depth")
    up = [(i, i + 1) for i in range(lax.axis_size("depth") - 1)]
    up_t = [(i, i + 1) for i in range(lax.axis_size("tile") - 1)]
    front = lax.ppermute(volume[slabs - 1], "depth", up)
    back = lax.ppermute(volume[0], "depth", [(b, a) for a, b in up])
    above = lax.ppermute(volume[:, rows - 1 :], "tile", up_t)
    below = lax.ppermute(volume[:, :1], "tile", [(b, a) for a, b in up_t])
    base = jnp.full((1,), lax.axis_index("depth") * slabs, jnp.int32)
    parts = cast(volume, front, back, above, below, entry_depth, light_dir, transfer, base, float(slabs * groups))
    parts = lax.all_to_all(parts, "depth", 0, 0)
    return merge(parts)


def solution(mesh):
    placed = (P("depth", "tile", None), P("tile", None), P(), P())
    return jax.shard_map(
        local, mesh=mesh, in_specs=placed, out_specs=P(None, "tile", "depth"), check_vma=False
    )
```

time: 196 us -> 95.3 us (0.49)
  other arithmetic: 99.9 us -> 0 us
  waiting for transfers between devices: 53 us -> 4.77 us
  blocking collectives: 0 us -> 37.3 us
  Pallas kernels: 0 us -> 33.8 us
  starting transfers between devices: 22.8 us -> 10.2 us
  local copies, waits for them, and re-layouts: 16.8 us -> 8.76 us
  between operations: 2.87 us -> 0.07 us
    another operation x3 -> x0, other arithmetic: 67.7 us -> none  [the longest x2 47.5 us: emission(): jnp.stack([shading * jax.nn.sigmoid(transfer[k, 0] * centre + transfer[k,...]
    ppermute x8 -> x4, waiting for transfers between devices: 53 us -> 4.77 us  [the longest x1 3.79 us: local(): above = lax.ppermute(volume[:, rows - 1:], 'tile', up_t)]
    all_to_all x0 -> x1, blocking collectives: none -> 37.3 us  [local(): parts = lax.all_to_all(parts, 'depth', 0, 0)]
    pallas_call x0 -> x2, Pallas kernels: none -> 33.8 us  [the longest x1 28.6 us: cast(): pl.pallas_call(functools.partial(cast_kernel, depth_total), grid=(rows //...]
    reduce_sum x2 -> x0, other arithmetic: 13.4 us -> none  [the longest x1 12.1 us: composite(): shaded = jnp.sum(weight[None] * colors, axis=1)]
    ppermute x8 -> x4, starting transfers between devices: 22.8 us -> 10.2 us  [the longest x1 4.58 us: local(): front = lax.ppermute(volume[slabs - 1], 'depth', up)]
    concatenate x1 -> x0, other arithmetic: 12.2 us -> none  [padded_2(): jnp.concatenate([lax.ppermute(tail, axis, [(i, (i + 1) % count) for i in...]
    slice x1 -> x0, other arithmetic: 5.11 us -> none  [local(): upper = halves[:, :, :, 1]]
  transfers between devices with their start and end apart: 8 -> 4, of which waited for: 7 -> 3; matrix products, arithmetic and copies ran while one was open for 4% -> 2% of each run, Pallas kernels for 0% -> 0%
where the time goes in v1:
time: 95.3 us; the launch traced here: 94.8 us
  blocking collectives  37.3 us (39%)
  Pallas kernels  33.8 us (35%)
  starting transfers between devices  10.2 us (11%)
  local copies, waits for them, and re-layouts  8.76 us (9%)
  waiting for transfers between devices  4.77 us (5%)
    all_to_all x1, blocking collectives, local(): parts = lax.all_to_all(parts, 'depth', 0, 0)  37.3 us
    pallas_call x1, Pallas kernels, cast(): pl.pallas_call(functools.partial(cast_kernel, depth_total), grid=(rows //...  28.6 us
    unnamed x8, local copies, waits for them, and re-layouts  5.76 us
    pallas_call x1, Pallas kernels, merge(): pl.pallas_call(merge_kernel, grid=(rows // ROW,), in_specs=[pl.BlockSpec(...  5.19 us
    ppermute x1, starting transfers between devices, local(): front = lax.ppermute(volume[slabs - 1], 'depth', up)  4.58 us
    ppermute x1, waiting for transfers between devices, local(): above = lax.ppermute(volume[:, rows - 1:], 'tile', up_t)  3.79 us
    ppermute x1, starting transfers between devices, local(): above = lax.ppermute(volume[:, rows - 1:], 'tile', up_t)  2.41 us
    ppermute x1, starting transfers between devices, local(): below = lax.ppermute(volume[:, :1], 'tile', [(b, a) for a, b in up_t])  1.92 us
  transfers between devices with their start and end apart: 4, of which 3 were waited for; matrix products, arithmetic and copies ran while one was open for 2% of the time, Pallas kernels for 0%

profile of v1, /device:TPU:96, one launch (start us, length us, event | category | flops | bytes accessed | tf_op | source)
XLA Modules:
  0.0 94.8 jit_solution(10678786418944914872)
XLA Ops:
  0.0 1.3 %slice_bitcast_fusion = (f32[64,2048]{1,0:T(8,128)S(1)}, f32[64,2048]{1,0:T(8,128)S(1)}) fusion(f32[16,64,2048]{2,1,0:T(8,128)} %volume.1), kind=kLoop, calls=%fused_computation | loop fusion | bytes 2097152 | tf_op jit(solution)/shard_map/squeeze | solution.py:176
  1.3 1.3 %collective-permute-start.1 = (f32[64,2048]{1,0:T(8,128)S(1)}, f32[64,2048]{1,0:T(8,128)S(1)}, u32[]{:S(2)}, u32[]{:S(2)}) collective-permute-start(f32[64,2048]{1,0:T(8,128)S(1)} %get-tuple-element.7), channel_id=1, source_target_pairs={{16,0},{32,16},{48,32},{64,48},{80,64},{96,80},{112,96},{128,112},... | collective-permute-start | bytes 1572872 | tf_op jit(solution)/shard_map/ppermute | solution.py:176
  2.6 4.6 %collective-permute-start = (f32[64,2048]{1,0:T(8,128)S(1)}, f32[64,2048]{1,0:T(8,128)S(1)}, u32[]{:S(2)}, u32[]{:S(2)}) collective-permute-start(f32[64,2048]{1,0:T(8,128)S(1)} %get-tuple-element.8), channel_id=1, source_target_pairs={{0,16},{16,32},{32,48},{48,64},{64,80},{80,96},{96,112},{112,128},... | collective-permute-start | bytes 1572872 | tf_op jit(solution)/shard_map/ppermute | solution.py:175
  7.2 1.7 %fusion = (f32[16,1,2048]{2,1,0:T(1,128)S(1)}, f32[16,1,2048]{2,1,0:T(1,128)S(1)}) fusion(f32[16,64,2048]{2,1,0:T(8,128)} %volume.1), kind=kLoop, calls=%fused_computation.2 | loop fusion | bytes 524288 | tf_op jit(solution)/shard_map/slice | solution.py:178
  8.9 1.9 %collective-permute-start.3 = (f32[16,1,2048]{2,1,0:T(1,128)S(1)}, f32[16,1,2048]{2,1,0:T(1,128)S(1)}, u32[]{:S(2)}, u32[]{:S(2)}) collective-permute-start(f32[16,1,2048]{2,1,0:T(1,128)S(1)} %get-tuple-element.5), channel_id=1, source_target_pairs={{1,0},{2,1},{3,2},{4,3},{5,4},{6,5},{7,6},{8,7},{9,8},{10,9},{11,1... | collective-permute-start | bytes 393224 | tf_op jit(solution)/shard_map/ppermute | solution.py:178
  10.8 2.4 %collective-permute-start.2 = (f32[16,1,2048]{2,1,0:T(1,128)S(1)}, f32[16,1,2048]{2,1,0:T(1,128)S(1)}, u32[]{:S(2)}, u32[]{:S(2)}) collective-permute-start(f32[16,1,2048]{2,1,0:T(1,128)S(1)} %get-tuple-element.6), channel_id=1, source_target_pairs={{0,1},{1,2},{2,3},{3,4},{4,5},{5,6},{6,7},{7,8},{8,9},{9,10},{10,1... | collective-permute-start | bytes 393224 | tf_op jit(solution)/shard_map/ppermute | solution.py:177
  13.2 0.1 collective-permute-done.3.below
  13.3 3.8 %collective-permute-done.2.above = f32[16,1,2048]{2,1,0:T(1,128)S(1)} collective-permute-done((f32[16,1,2048]{2,1,0:T(1,128)S(1)}, f32[16,1,2048]{2,1,0:T(1,128)S(1)}, u32[]{:S(2)}, u32[]{:S(2)}) %collective-permute-start.2) | collective-permute-done | bytes 131104 | tf_op jit(solution)/shard_map/ppermute | solution.py:177
  17.1 0.0 collective-permute-done.1.back
  17.1 0.9 collective-permute-done.front
  18.0 0.0 copy-start
  18.0 3.4 %copy-done = f32[16,64,2048]{2,1,0:T(8,128)S(1)} copy-done((f32[16,64,2048]{2,1,0:T(8,128)S(1)}, f32[16,64,2048]{2,1,0:T(8,128)}, u32[]{:S(2)}) %copy-start) | copy-done | bytes 8388632
  21.4 0.0 copy-start.1
  21.4 1.0 %copy-done.1 = s32[64,2048]{1,0:T(8,128)S(1)} copy-done((s32[64,2048]{1,0:T(8,128)S(1)}, s32[64,2048]{1,0:T(8,128)}, u32[]{:S(2)}) %copy-start.1) | copy-done | bytes 524312
  22.4 0.0 copy-start.2
  22.4 0.7 copy-done.2
  23.1 0.0 copy-start.3
  23.1 0.7 copy-done.3
  23.8 28.6 %cast.1 = f32[16,4,64,128]{3,2,1,0:T(8,128)S(1)} custom-call(f32[3]{0:T(128)S(1)} %copy-done.3, f32[4,3]{1,0:T(4,128)S(1)} %copy-done.2, s32[1]{0:T(128)} %bitcast.base, f32[16,64,2048]{2,1,0:T(8,128)S(1)} %copy-done, f32[64,2048]{1,0:T(8,128)S(1)} %collective-permute-done.front, f32[64,2048]{1,0:T(8,128)S(1)} %collective-permute-done.1.back, ...), custom_call_target="tpu_custom_call" | custom-call | flops 125829120 | bytes 10485760 | tf_op jit(solution)/shard_map/cast/pallas_call | solution.py:131
  52.4 37.3 %all_to_all.5.parts = f32[16,4,64,128]{3,2,1,0:T(8,128)} all-to-all(f32[16,4,64,128]{3,2,1,0:T(8,128)S(1)} %cast.1), channel_id=1, replica_groups=mesh['depth'=16,'tile'=16] {'depth'}, dimensions={0} | all-to-all | bytes 4194304 | tf_op jit(solution)/shard_map/all_to_all | solution.py:181
  89.6 5.2 %merge.1 = f32[4,64,128]{2,1,0:T(8,128)} custom-call(f32[16,4,64,128]{3,2,1,0:T(8,128)} %all_to_all.5.parts), custom_call_target="tpu_custom_call" | custom-call | tf_op jit(solution)/shard_map/merge/pallas_call | solution.py:160
Async XLA Ops:
  1.3 15.8 %collective-permute-start.1 = (f32[64,2048]{1,0:T(8,128)S(1)}, f32[64,2048]{1,0:T(8,128)S(1)}, u32[]{:S(2)}, u32[]{:S(2)}) collective-permute-start(f32[64,2048]{1,0:T(8,128)S(1)} %get-tuple-element.7), channel_id=1, source_target_pairs={{16,0},{32,16},{48,32},{64,48},{80,64},{96,80},{112,96},{128,112},... | collective-permute-start | bytes 1572872 | tf_op jit(solution)/shard_map/ppermute | solution.py:176
  2.6 15.4 %collective-permute-start = (f32[64,2048]{1,0:T(8,128)S(1)}, f32[64,2048]{1,0:T(8,128)S(1)}, u32[]{:S(2)}, u32[]{:S(2)}) collective-permute-start(f32[64,2048]{1,0:T(8,128)S(1)} %get-tuple-element.8), channel_id=1, source_target_pairs={{0,16},{16,32},{32,48},{48,64},{64,80},{80,96},{96,112},{112,128},... | collective-permute-start | bytes 1572872 | tf_op jit(solution)/shard_map/ppermute | solution.py:175
  8.9 4.4 %collective-permute-start.3 = (f32[16,1,2048]{2,1,0:T(1,128)S(1)}, f32[16,1,2048]{2,1,0:T(1,128)S(1)}, u32[]{:S(2)}, u32[]{:S(2)}) collective-permute-start(f32[16,1,2048]{2,1,0:T(1,128)S(1)} %get-tuple-element.5), channel_id=1, source_target_pairs={{1,0},{2,1},{3,2},{4,3},{5,4},{6,5},{7,6},{8,7},{9,8},{10,9},{11,1... | collective-permute-start | bytes 393224 | tf_op jit(solution)/shard_map/ppermute | solution.py:178
  10.8 6.3 %collective-permute-start.2 = (f32[16,1,2048]{2,1,0:T(1,128)S(1)}, f32[16,1,2048]{2,1,0:T(1,128)S(1)}, u32[]{:S(2)}, u32[]{:S(2)}) collective-permute-start(f32[16,1,2048]{2,1,0:T(1,128)S(1)} %get-tuple-element.6), channel_id=1, source_target_pairs={{0,1},{1,2},{2,3},{3,4},{4,5},{5,6},{6,7},{7,8},{8,9},{9,10},{10,1... | collective-permute-start | bytes 393224 | tf_op jit(solution)/shard_map/ppermute | solution.py:177
  18.0 3.4 %copy-start = (f32[16,64,2048]{2,1,0:T(8,128)S(1)}, f32[16,64,2048]{2,1,0:T(8,128)}, u32[]{:S(2)}) copy-start(f32[16,64,2048]{2,1,0:T(8,128)} %volume.1) | copy-start | bytes 25165828
  21.4 1.0 %copy-start.1 = (s32[64,2048]{1,0:T(8,128)S(1)}, s32[64,2048]{1,0:T(8,128)}, u32[]{:S(2)}) copy-start(s32[64,2048]{1,0:T(8,128)} %entry.1) | copy-start | bytes 1572868
  22.4 0.7 copy-start.2
  23.1 0.7 copy-start.3

commit v2 on v0

v2 whole, which is shorter than its diff:
```python
import functools

import jax
import jax.numpy as jnp
from jax import lax
from jax.experimental import pallas as pl
from jax.experimental.pallas import tpu as pltpu
from jax.sharding import PartitionSpec as P

ROW = 8
LANE = 128
LOG2E = 1.4426950408889634
CHANNELS = 4
VMEM = pl.BlockSpec(memory_space=pltpu.VMEM)
SMEM = pl.BlockSpec(memory_space=pltpu.SMEM)
HBM = pl.BlockSpec(memory_space=pl.ANY)


def edges_kernel(volume, last_slab, first_slab, last_row, first_row, sems):
    slabs, rows, _ = volume.shape
    copies = [
        pltpu.make_async_copy(volume.at[slabs - 1], last_slab, sems.at[0]),
        pltpu.make_async_copy(volume.at[0], first_slab, sems.at[1]),
        pltpu.make_async_copy(volume.at[:, pl.ds(rows - 1, 1), :], last_row, sems.at[2]),
        pltpu.make_async_copy(volume.at[:, pl.ds(0, 1), :], first_row, sems.at[3]),
    ]
    for copy in copies:
        copy.start()
    for copy in copies:
        copy.wait()


def edges(volume):
    slabs, rows, columns = volume.shape
    slab = jax.ShapeDtypeStruct((rows, columns), jnp.float32)
    row = jax.ShapeDtypeStruct((slabs, 1, columns), jnp.float32)
    return pl.pallas_call(
        edges_kernel,
        in_specs=[HBM],
        out_specs=[VMEM] * 4,
        out_shape=[slab, slab, row, row],
        scratch_shapes=[pltpu.SemaphoreType.DMA((4,))],
        compiler_params=pltpu.CompilerParams(vmem_limit_bytes=50 * 2**20),
        cost_estimate=pl.CostEstimate(flops=0, bytes_accessed=4 * 2**20, transcendentals=0),
        name="edges",
    )(volume)


def constants(light, transfer, depth_total):
    def splat(value):
        return jnp.full((ROW, LANE), value, jnp.float32)

    toward = [splat(light[i]) for i in range(3)]
    scale = 0.35 * lax.rsqrt(toward[0] * toward[0] + toward[1] * toward[1] + toward[2] * toward[2])
    toward = [value * scale for value in toward]
    hues = [
        (splat(transfer[k, 0] * 0.5), splat(transfer[k, 1] * 0.25), splat(transfer[k, 2] * 0.5))
        for k in range(3)
    ]
    veil = (
        splat(transfer[3, 0] * -LOG2E),
        splat(transfer[3, 1] * (-0.5 * LOG2E)),
        splat(transfer[3, 2] * -LOG2E) + jnp.log2(splat(depth_total / 4.0)),
    )
    return toward, hues, veil


class Shader:
    def __init__(self, light, transfer, depth_total):
        self.toward, self.hues, self.veil = constants(light, transfer, depth_total)
        self.bound = depth_total / 4.0

    def lateral(self, gx, gy):
        return gx * gx + gy * gy + 4.0, self.toward[1] * gx + self.toward[2] * gy

    def add(self, state, visible, here, gz, square, facing):
        alpha, plain, tinted = state
        square = square + gz * gz
        inverse = lax.rsqrt(square)
        norm = square * inverse
        shade = 0.15 + jnp.abs(self.toward[0] * gz + facing) * inverse
        dim = jnp.exp2(self.veil[0] * here + self.veil[1] * norm + self.veil[2])
        root = lax.rsqrt(dim + self.bound)
        opacity = jnp.where(visible, root * root, 0.0)
        weight = opacity - alpha * opacity
        lit = weight * shade
        tinted = [
            tinted[k] + lit * jnp.tanh(self.hues[k][0] * here + self.hues[k][1] * norm + self.hues[k][2])
            for k in range(3)
        ]
        return alpha + weight, plain + lit, tinted


class Bricks:
    def __init__(self, cells, lanes):
        self.cells = cells
        self.left_edge, self.right_edge = lanes == 0, lanes == LANE - 1

    def load(self, piece, slab, at, shift=0, aside=0):
        return self.cells[piece + 1 + aside, slab, pl.ds(at + shift, ROW), :]

    def lateral(self, shader, piece, slab, at, here):
        lf = pltpu.roll(jnp.where(self.right_edge, self.load(piece, slab, at, 0, -1), here), 1, 1)
        rt = pltpu.roll(jnp.where(self.left_edge, self.load(piece, slab, at, 0, 1), here), LANE - 1, 1)
        return shader.lateral(self.load(piece, slab, at, 1) - self.load(piece, slab, at, -1), rt - lf)

    def clear_sides(self, at, rows):
        pieces, slabs = self.cells.shape[0] - 2, self.cells.shape[1]
        blank = jnp.zeros((rows, LANE), jnp.float32)
        for slab in range(slabs):
            self.cells[0, slab, at : at + rows] = blank
            self.cells[pieces + 1, slab, at : at + rows] = blank


def middle_kernel(depth_total, light, transfer, base, volume, entry, seen, ends, cells, sems):
    slabs, rows, columns = volume.shape
    pieces = columns // LANE

    def fetch(piece):
        return pltpu.make_async_copy(
            volume.at[:, :, pl.ds(pl.multiple_of(piece * LANE, LANE), LANE)],
            cells.at[piece + 1],
            sems.at[piece],
        )

    def begin(piece, carry):
        fetch(piece).start()
        return carry

    lax.fori_loop(0, pieces, begin, 0)
    bricks = Bricks(cells, lax.broadcasted_iota(jnp.int32, (ROW, LANE), 1))
    bricks.clear_sides(ROW, rows - 2 * ROW)
    shader = Shader(light, transfer, depth_total)
    origin = base[0]
    zero = jnp.zeros((ROW, LANE), jnp.float32)
    fetch(0).wait()

    def column(piece, carry):
        @pl.when(piece < pieces - 1)
        def _():
            fetch(piece + 1).wait()

        cols = pl.ds(pl.multiple_of(piece * LANE, LANE), LANE)
        for at in range(ROW, rows - ROW, ROW):
            start = entry[at : at + ROW, cols] - origin
            state = (zero, zero, [zero] * 3)
            before, here = bricks.load(piece, 0, at), bricks.load(piece, 1, at)
            for slab in range(1, slabs - 1):
                after = bricks.load(piece, slab + 1, at)
                side = bricks.lateral(shader, piece, slab, at, here)
                state = shader.add(state, start <= slab, here, after - before, *side)
                before, here = here, after
            to = pl.ds(at - ROW, ROW)
            for k in range(3):
                seen[piece, k, to, :] = state[1] + state[2][k]
            seen[piece, 3, to, :] = state[0]
            for end, (slab, inner) in enumerate(((0, 1), (slabs - 1, slabs - 2))):
                side = bricks.lateral(shader, piece, slab, at, bricks.load(piece, slab, at))
                for k, value in enumerate((*side, bricks.load(piece, inner, at))):
                    ends[end, k, piece, to, :] = value
        return carry

    lax.fori_loop(0, pieces, column, 0)


def finish_kernel(
    depth_total, light, transfer, base, volume, entry, above, below, front, back, near, far, seen, ends, out, upper, lower, sems
):
    slabs, rows, columns = volume.shape
    pieces = columns // LANE
    at_last = rows - ROW

    def fetches(piece):
        cols = pl.ds(pl.multiple_of(piece * LANE, LANE), LANE)
        return (
            pltpu.make_async_copy(
                volume.at[:, pl.ds(0, 2 * ROW), cols], upper.at[piece + 1, :, pl.ds(ROW, 2 * ROW), :], sems.at[0, piece]
            ),
            pltpu.make_async_copy(
                volume.at[:, pl.ds(rows - 2 * ROW, 2 * ROW), cols], lower.at[piece + 1, :, pl.ds(0, 2 * ROW), :], sems.at[1, piece]
            ),
        )

    def begin(piece, carry):
        for copy in fetches(piece):
            copy.start()
        return carry

    lax.fori_loop(0, pieces, begin, 0)
    shader = Shader(light, transfer, depth_total)
    lanes = lax.broadcasted_iota(jnp.int32, (ROW, LANE), 1)
    tops, bottoms = Bricks(upper, lanes), Bricks(lower, lanes)
    for bricks in (tops, bottoms):
        bricks.clear_sides(ROW, ROW)
    origin = base[0]
    zero = jnp.zeros((ROW, LANE), jnp.float32)

    def closing(piece, carry):
        cols = pl.ds(pl.multiple_of(piece * LANE, LANE), LANE)
        for row in range(ROW, at_last, ROW):
            at, src = pl.ds(row, ROW), pl.ds(row - ROW, ROW)
            start = entry[at, cols] - origin
            square, facing, inner = (ends[0, k, piece, src, :] for k in range(3))
            alpha, plain, tinted = shader.add(
                (zero, zero, [zero] * 3), start <= 0, near[at, cols], inner - front[at, cols], square, facing
            )
            clear = 1.0 - alpha
            tinted = [tinted[k] + plain + clear * seen[piece, k, src, :] for k in range(3)]
            alpha = alpha + clear * seen[piece, 3, src, :]
            square, facing, inner = (ends[1, k, piece, src, :] for k in range(3))
            alpha, plain, tinted = shader.add(
                (alpha, zero, tinted), start <= slabs - 1, far[at, cols], back[at, cols] - inner, square, facing
            )
            for k in range(3):
                out[piece, k, at, :] = plain + tinted[k]
            out[piece, 3, at, :] = alpha
        return carry

    lax.fori_loop(0, pieces, closing, 0)

    def ready(piece, carry):
        for copy in fetches(piece):
            copy.wait()
        cols = pl.ds(pl.multiple_of(piece * LANE, LANE), LANE)
        for slab in range(slabs):
            upper[piece + 1, slab, ROW - 1 : ROW, :] = above[slab, :, cols]
            lower[piece + 1, slab, 2 * ROW : 2 * ROW + 1, :] = below[slab, :, cols]
        return carry

    lax.fori_loop(0, pieces, ready, 0)

    def rims(piece, carry):
        cols = pl.ds(pl.multiple_of(piece * LANE, LANE), LANE)
        for bricks, row in ((tops, 0), (bottoms, at_last)):
            at = pl.ds(row, ROW)
            start = entry[at, cols] - origin
            alpha, plain, tinted = zero, zero, [zero] * 3
            before, here = front[at, cols], bricks.load(piece, 0, ROW)
            for slab in range(slabs):
                after = back[at, cols] if slab == slabs - 1 else bricks.load(piece, slab + 1, ROW)
                side = bricks.lateral(shader, piece, slab, ROW, here)
                alpha, plain, tinted = shader.add((alpha, plain, tinted), start <= slab, here, after - before, *side)
                before, here = here, after
            for k in range(3):
                out[piece, k, at, :] = plain + tinted[k]
            out[piece, 3, at, :] = alpha
        return carry

    lax.fori_loop(0, pieces, rims, 0, unroll=2)


def middle(volume, entry, light, transfer, base, depth_total):
    slabs, rows, columns = volume.shape
    pieces, inner = columns // LANE, rows - 2 * ROW
    work = (slabs - 2) * inner * columns
    return pl.pallas_call(
        functools.partial(middle_kernel, depth_total),
        in_specs=[SMEM, SMEM, SMEM, HBM, VMEM],
        out_specs=[VMEM, VMEM],
        out_shape=[
            jax.ShapeDtypeStruct((pieces, CHANNELS, inner, LANE), jnp.float32),
            jax.ShapeDtypeStruct((2, 3, pieces, inner, LANE), jnp.float32),
        ],
        scratch_shapes=[
            pltpu.VMEM((pieces + 2, slabs, rows, LANE), jnp.float32),
            pltpu.SemaphoreType.DMA((pieces,)),
        ],
        compiler_params=pltpu.CompilerParams(vmem_limit_bytes=46 * 2**20),
        cost_estimate=pl.CostEstimate(flops=work * 60, bytes_accessed=work * 4, transcendentals=work * 6),
        name="middle",
    )(light, transfer, base, volume, entry)


def finish(volume, entry, above, below, front, back, near, far, seen, ends, light, transfer, base, depth_total):
    slabs, rows, columns = volume.shape
    pieces = columns // LANE
    work = slabs * 2 * ROW * columns + 2 * rows * columns
    rim = pltpu.VMEM((pieces + 2, slabs, 3 * ROW, LANE), jnp.float32)
    return pl.pallas_call(
        functools.partial(finish_kernel, depth_total),
        in_specs=[SMEM] * 3 + [HBM] + [VMEM] * 9,
        out_specs=VMEM,
        out_shape=jax.ShapeDtypeStruct((pieces, CHANNELS, rows, LANE), jnp.float32),
        scratch_shapes=[rim, rim, pltpu.SemaphoreType.DMA((2, pieces))],
        compiler_params=pltpu.CompilerParams(vmem_limit_bytes=40 * 2**20),
        cost_estimate=pl.CostEstimate(flops=work * 60, bytes_accessed=work * 4, transcendentals=work * 6),
        name="finish",
    )(light, transfer, base, volume, entry, above, below, front, back, near, far, seen, ends)


def merge_kernel(parts, out):
    count, _, rows, _ = parts.shape

    def rows_of(tile, carry):
        at = pl.ds(pl.multiple_of(tile * ROW, ROW), ROW)
        clear = 1.0 - parts[0, 3, at, :]
        total = [parts[0, k, at, :] for k in range(CHANNELS)]
        for d in range(1, count):
            total = [total[k] + clear * parts[d, k, at, :] for k in range(CHANNELS)]
            clear = clear - clear * parts[d, 3, at, :]
        for k in range(CHANNELS):
            out[k, at, :] = total[k]
        return carry

    lax.fori_loop(0, rows // ROW, rows_of, 0, unroll=2)


def merge(parts):
    _, channels, rows, cols = parts.shape
    return pl.pallas_call(
        merge_kernel,
        in_specs=[VMEM],
        out_specs=VMEM,
        out_shape=jax.ShapeDtypeStruct((channels, rows, cols), jnp.float32),
        compiler_params=pltpu.CompilerParams(vmem_limit_bytes=8 * 2**20),
        cost_estimate=pl.CostEstimate(flops=parts.size, bytes_accessed=parts.size * 4, transcendentals=0),
        name="merge",
    )(parts)


def local(volume, entry, light, transfer):
    slabs, _, _ = volume.shape
    groups, tiles = lax.axis_size("depth"), lax.axis_size("tile")
    total = float(slabs * groups)
    up = [(i, i + 1) for i in range(groups - 1)]
    up_t = [(i, i + 1) for i in range(tiles - 1)]
    last_slab, first_slab, last_row, first_row = edges(volume)
    front = lax.ppermute(last_slab, "depth", up)
    back = lax.ppermute(first_slab, "depth", [(b, a) for a, b in up])
    above = lax.ppermute(last_row, "tile", up_t)
    below = lax.ppermute(first_row, "tile", [(b, a) for a, b in up_t])
    base = jnp.full((1,), lax.axis_index("depth") * slabs, jnp.int32)

    seen, ends = middle(volume, entry, light, transfer, base, total)
    parts = finish(
        volume, entry, above, below, front, back, first_slab, last_slab, seen, ends, light, transfer, base, total
    )
    return merge(lax.all_to_all(parts, "depth", 0, 0))


def solution(mesh):
    placed = (P("depth", "tile", None), P("tile", None), P(), P())
    return jax.shard_map(local, mesh=mesh, in_specs=placed, out_specs=P(None, "tile", "depth"), check_vma=False)
```

time: 196 us -> 71.7 us (0.37)
  other arithmetic: 99.9 us -> 0 us
  waiting for transfers between devices: 53 us -> 0.01 us
  blocking collectives: 0 us -> 37.2 us
  Pallas kernels: 0 us -> 23.3 us
  local copies, waits for them, and re-layouts: 16.8 us -> 0.01 us
  starting transfers between devices: 22.8 us -> 10.4 us
  between operations: 2.87 us -> 0.12 us
    another operation x3 -> x0, other arithmetic: 67.7 us -> none  [the longest x2 47.5 us: emission(): jnp.stack([shading * jax.nn.sigmoid(transfer[k, 0] * centre + transfer[k,...]
    ppermute x8 -> x4, waiting for transfers between devices: 53 us -> 0.01 us  [the longest x1 0.01 us: local(): below = lax.ppermute(first_row, 'tile', [(b, a) for a, b in up_t])]
    all_to_all x0 -> x1, blocking collectives: none -> 37.2 us  [local(): return merge(lax.all_to_all(parts, 'depth', 0, 0))]
    pallas_call x0 -> x4, Pallas kernels: none -> 23.3 us  [the longest x1 13.5 us: middle(): pl.pallas_call(functools.partial(middle_kernel, depth_total), in_specs=[S...]
    reduce_sum x2 -> x0, other arithmetic: 13.4 us -> none  [the longest x1 12.1 us: composite(): shaded = jnp.sum(weight[None] * colors, axis=1)]
    ppermute x8 -> x4, starting transfers between devices: 22.8 us -> 10.4 us  [the longest x1 3.64 us: local(): below = lax.ppermute(first_row, 'tile', [(b, a) for a, b in up_t])]
    concatenate x1 -> x0, other arithmetic: 12.2 us -> none  [padded_2(): jnp.concatenate([lax.ppermute(tail, axis, [(i, (i + 1) % count) for i in...]
    unnamed x13 -> x6, local copies, waits for them, and re-layouts: 9.29 us -> 0.01 us
  transfers between devices with their start and end apart: 8 -> 4, of which waited for: 7 -> 0; matrix products, arithmetic and copies ran while one was open for 4% -> 0% of each run, Pallas kernels for 0% -> 19%
where the time goes in v2:
time: 71.7 us; the launch traced here: 71.1 us
  blocking collectives  37.2 us (52%)
  Pallas kernels  23.3 us (32%)
  starting transfers between devices  10.4 us (15%)
    all_to_all x1, blocking collectives, local(): return merge(lax.all_to_all(parts, 'depth', 0, 0))  37.2 us
    pallas_call x1, Pallas kernels, middle(): pl.pallas_call(functools.partial(middle_kernel, depth_total), in_specs=[S...  13.5 us
    pallas_call x1, Pallas kernels, finish(): pl.pallas_call(functools.partial(finish_kernel, depth_total), in_specs=[S...  7.66 us
    ppermute x1, starting transfers between devices, local(): below = lax.ppermute(first_row, 'tile', [(b, a) for a, b in up_t])  3.64 us
    ppermute x1, starting transfers between devices, local(): front = lax.ppermute(last_slab, 'depth', up)  3.51 us
    ppermute x1, starting transfers between devices, local(): above = lax.ppermute(last_row, 'tile', up_t)  1.92 us
  transfers between devices with their start and end apart: 4, of which 0 were waited for; matrix products, arithmetic and copies ran while one was open for 0% of the time, Pallas kernels for 19%

profile of v2, /device:TPU:96, one launch (start us, length us, event | category | flops | bytes accessed | tf_op | source)
XLA Modules:
  0.0 71.1 jit_solution(2110311348625008947)
XLA Ops:
  0.0 0.0 copy-start.1
  0.0 0.0 copy-start.2
  0.0 0.0 copy-start
  0.0 1.4 %edges.1 = (f32[64,2048]{1,0:T(8,128)S(1)}, f32[64,2048]{1,0:T(8,128)S(1)}, f32[16,1,2048]{2,1,0:T(1,128)S(1)}, f32[16,1,2048]{2,1,0:T(1,128)S(1)}) custom-call(f32[16,64,2048]{2,1,0:T(8,128)} %volume.5), custom_call_target="tpu_custom_call" | custom-call | bytes 4194304 | tf_op jit(solution)/shard_map/edges/pallas_call | solution.py:37
  1.4 3.5 %collective-permute-start.2 = (f32[64,2048]{1,0:T(8,128)S(1)}, f32[64,2048]{1,0:T(8,128)S(1)}, u32[]{:S(2)}, u32[]{:S(2)}) collective-permute-start(f32[64,2048]{1,0:T(8,128)S(1)} %get-tuple-element.13.far), channel_id=1, source_target_pairs={{0,16},{16,32},{32,48},{48,64},{64,80},{80,96},{96,112},{112,128},... | collective-permute-start | bytes 1572872 | tf_op jit(solution)/shard_map/ppermute | solution.py:328
  4.9 1.3 %collective-permute-start.3 = (f32[64,2048]{1,0:T(8,128)S(1)}, f32[64,2048]{1,0:T(8,128)S(1)}, u32[]{:S(2)}, u32[]{:S(2)}) collective-permute-start(f32[64,2048]{1,0:T(8,128)S(1)} %get-tuple-element.14.near), channel_id=1, source_target_pairs={{16,0},{32,16},{48,32},{64,48},{80,64},{96,80},{112,96},{128,112},... | collective-permute-start | bytes 1572872 | tf_op jit(solution)/shard_map/ppermute | solution.py:329
  6.2 1.9 %collective-permute-start = (f32[16,1,2048]{2,1,0:T(1,128)S(1)}, f32[16,1,2048]{2,1,0:T(1,128)S(1)}, u32[]{:S(2)}, u32[]{:S(2)}) collective-permute-start(f32[16,1,2048]{2,1,0:T(1,128)S(1)} %get-tuple-element.11), channel_id=1, source_target_pairs={{0,1},{1,2},{2,3},{3,4},{4,5},{5,6},{6,7},{7,8},{8,9},{9,10},{10,1... | collective-permute-start | bytes 393224 | tf_op jit(solution)/shard_map/ppermute | solution.py:330
  8.1 3.6 %collective-permute-start.1 = (f32[16,1,2048]{2,1,0:T(1,128)S(1)}, f32[16,1,2048]{2,1,0:T(1,128)S(1)}, u32[]{:S(2)}, u32[]{:S(2)}) collective-permute-start(f32[16,1,2048]{2,1,0:T(1,128)S(1)} %get-tuple-element.12), channel_id=1, source_target_pairs={{1,0},{2,1},{3,2},{4,3},{5,4},{6,5},{7,6},{8,7},{9,8},{10,9},{11,1... | collective-permute-start | bytes 393224 | tf_op jit(solution)/shard_map/ppermute | solution.py:331
  11.8 0.0 copy-done.1
  11.8 0.0 copy-done.2
  11.8 0.0 copy-done
  11.8 13.5 %middle.1 = (f32[16,4,48,128]{3,2,1,0:T(8,128)S(1)}, f32[2,3,16,48,128]{4,3,2,1,0:T(8,128)S(1)}) custom-call(f32[3]{0:T(128)S(1)} %copy-done.2, f32[4,3]{1,0:T(4,128)S(1)} %copy-done.1, s32[1]{0:T(128)} %bitcast.base, f32[16,64,2048]{2,1,0:T(8,128)} %volume.5, s32[64,2048]{1,0:T(8,128)S(1)} %copy-done), custom_call_target="tpu_custom_call" | custom-call | flops 82575360 | bytes 5505024 | tf_op jit(solution)/shard_map/middle/pallas_call | solution.py:256
  25.3 0.0 collective-permute-done.above
  25.3 0.0 collective-permute-done.1.below
  25.3 0.0 collective-permute-done.2.front
  25.3 0.0 collective-permute-done.3.back
  25.3 7.7 %finish.1 = f32[16,4,64,128]{3,2,1,0:T(8,128)S(1)} custom-call(f32[3]{0:T(128)S(1)} %copy-done.2, f32[4,3]{1,0:T(4,128)S(1)} %copy-done.1, s32[1]{0:T(128)} %bitcast.base, f32[16,64,2048]{2,1,0:T(8,128)} %volume.5, s32[64,2048]{1,0:T(8,128)S(1)} %copy-done, f32[16,1,2048]{2,1,0:T(1,128)S(1)} %collective-permute-done.above, ...), custom_call_target="tpu_custom_call" | custom-call | flops 47185920 | bytes 3145728 | tf_op jit(solution)/shard_map/finish/pallas_call | solution.py:279
  33.0 37.2 %all_to_all.5.parts = f32[16,4,64,128]{3,2,1,0:T(8,128)S(1)} all-to-all(f32[16,4,64,128]{3,2,1,0:T(8,128)S(1)} %finish.1), channel_id=1, replica_groups=mesh['depth'=16,'tile'=16] {'depth'}, dimensions={0} | all-to-all | bytes 4194304 | tf_op jit(solution)/shard_map/all_to_all | solution.py:338
  70.2 0.9 %merge.1 = f32[4,64,128]{2,1,0:T(8,128)} custom-call(f32[16,4,64,128]{3,2,1,0:T(8,128)S(1)} %all_to_all.5.parts), custom_call_target="tpu_custom_call" | custom-call | flops 524288 | bytes 2097152 | tf_op jit(solution)/shard_map/merge/pallas_call | solution.py:310
Async XLA Ops:
  0.0 11.8 %copy-start.1 = (f32[4,3]{1,0:T(4,128)S(1)}, f32[4,3]{1,0:T(4,128)}, u32[]{:S(2)}) copy-start(f32[4,3]{1,0:T(4,128)} %transfer.3) | copy-start | bytes 148
  0.0 11.8 %copy-start.2 = (f32[3]{0:T(128)S(1)}, f32[3]{0:T(128)}, u32[]{:S(2)}) copy-start(f32[3]{0:T(128)} %light.3) | copy-start | bytes 40
  0.0 11.8 %copy-start = (s32[64,2048]{1,0:T(8,128)S(1)}, s32[64,2048]{1,0:T(8,128)}, u32[]{:S(2)}) copy-start(s32[64,2048]{1,0:T(8,128)} %entry.3) | copy-start | bytes 1572868
  1.4 23.9 %collective-permute-start.2 = (f32[64,2048]{1,0:T(8,128)S(1)}, f32[64,2048]{1,0:T(8,128)S(1)}, u32[]{:S(2)}, u32[]{:S(2)}) collective-permute-start(f32[64,2048]{1,0:T(8,128)S(1)} %get-tuple-element.13.far), channel_id=1, source_target_pairs={{0,16},{16,32},{32,48},{48,64},{64,80},{80,96},{96,112},{112,128},... | collective-permute-start | bytes 1572872 | tf_op jit(solution)/shard_map/ppermute | solution.py:328
  4.9 20.4 %collective-permute-start.3 = (f32[64,2048]{1,0:T(8,128)S(1)}, f32[64,2048]{1,0:T(8,128)S(1)}, u32[]{:S(2)}, u32[]{:S(2)}) collective-permute-start(f32[64,2048]{1,0:T(8,128)S(1)} %get-tuple-element.14.near), channel_id=1, source_target_pairs={{16,0},{32,16},{48,32},{64,48},{80,64},{96,80},{112,96},{128,112},... | collective-permute-start | bytes 1572872 | tf_op jit(solution)/shard_map/ppermute | solution.py:329
  6.2 19.1 %collective-permute-start = (f32[16,1,2048]{2,1,0:T(1,128)S(1)}, f32[16,1,2048]{2,1,0:T(1,128)S(1)}, u32[]{:S(2)}, u32[]{:S(2)}) collective-permute-start(f32[16,1,2048]{2,1,0:T(1,128)S(1)} %get-tuple-element.11), channel_id=1, source_target_pairs={{0,1},{1,2},{2,3},{3,4},{4,5},{5,6},{6,7},{7,8},{8,9},{9,10},{10,1... | collective-permute-start | bytes 393224 | tf_op jit(solution)/shard_map/ppermute | solution.py:330
  8.1 17.2 %collective-permute-start.1 = (f32[16,1,2048]{2,1,0:T(1,128)S(1)}, f32[16,1,2048]{2,1,0:T(1,128)S(1)}, u32[]{:S(2)}, u32[]{:S(2)}) collective-permute-start(f32[16,1,2048]{2,1,0:T(1,128)S(1)} %get-tuple-element.12), channel_id=1, source_target_pairs={{1,0},{2,1},{3,2},{4,3},{5,4},{6,5},{7,6},{8,7},{9,8},{10,9},{11,1... | collective-permute-start | bytes 393224 | tf_op jit(solution)/shard_map/ppermute | solution.py:331

commit v3 on v2

--- a/solution.py
+++ b/solution.py
@@ -1,4 +1,5 @@
 import functools
+import math
 
 import jax
 import jax.numpy as jnp
@@ -46,48 +47,91 @@
     )(volume)
 
 
-def constants(light, transfer, depth_total):
+def constants(light, transfer):
     def splat(value):
         return jnp.full((ROW, LANE), value, jnp.float32)
 
     toward = [splat(light[i]) for i in range(3)]
     scale = 0.35 * lax.rsqrt(toward[0] * toward[0] + toward[1] * toward[1] + toward[2] * toward[2])
     toward = [value * scale for value in toward]
-    hues = [
-        (splat(transfer[k, 0] * 0.5), splat(transfer[k, 1] * 0.25), splat(transfer[k, 2] * 0.5))
-        for k in range(3)
-    ]
-    veil = (
-        splat(transfer[3, 0] * -LOG2E),
-        splat(transfer[3, 1] * (-0.5 * LOG2E)),
-        splat(transfer[3, 2] * -LOG2E) + jnp.log2(splat(depth_total / 4.0)),
-    )
-    return toward, hues, veil
+    rows = [[transfer[k, i] * (0.25 if i == 1 else 0.5) for i in range(3)] for k in range(3)]
+    rows.append([transfer[3, i] * (-0.5 * LOG2E if i == 1 else -LOG2E) for i in range(3)])
+    return toward, rows
+
+
+def mixing(rows, width):
+    size = (CHANNELS * ROW, 10 * ROW)
+    line = lax.broadcasted_iota(jnp.int32, size, 0)
+    column = lax.broadcasted_iota(jnp.int32, size, 1)
+    block, diagonal = column >> 3, (column & 7) == (line & 7)
+    shift = jnp.full(size, width, jnp.float32)
+
+    def chosen(i):
+        value = jnp.full(size, rows[0][i], jnp.float32)
+        for k in range(1, CHANNELS):
+            value = jnp.where(line >= k * ROW, rows[k][i], value)
+        return value
+
+    def top(value):
+        return value.astype(jnp.bfloat16).astype(jnp.float32)
+
+    scale = jnp.where((block & 1) == 0, chosen(0), chosen(1))
+    scale = jnp.where(block < 4, top(scale), scale - top(scale))
+    offset = chosen(2) + jnp.where(line >= 3 * ROW, shift, 0.0)
+    high = top(offset)
+    low = top(offset - high)
+    offset = jnp.where(column == 8 * ROW, high, jnp.where(column == 8 * ROW + 1, low, offset - high - low))
+    mix = jnp.where((block < 8) & diagonal, scale, jnp.where((column >= 8 * ROW) & (column < 8 * ROW + 3), offset, 0.0))
+    return mix.astype(jnp.bfloat16)
 
 
 class Shader:
     def __init__(self, light, transfer, depth_total):
-        self.toward, self.hues, self.veil = constants(light, transfer, depth_total)
+        self.toward, rows = constants(light, transfer)
         self.bound = depth_total / 4.0
+        width = math.log2(depth_total / 4.0)
+        self.rows = [
+            [jnp.full((ROW, LANE), row[i] + (width if (k, i) == (3, 2) else 0.0), jnp.float32) for i in range(3)]
+            for k, row in enumerate(rows)
+        ]
+        self.mix = mixing(rows, width)
+        self.ones = jnp.ones((2 * ROW, LANE), jnp.bfloat16)
 
     def lateral(self, gx, gy):
         return gx * gx + gy * gy + 4.0, self.toward[1] * gx + self.toward[2] * gy
 
-    def add(self, state, visible, here, gz, square, facing):
-        alpha, plain, tinted = state
+    def look(self, cells):
+        pairs, shades = [], []
+        for here, gz, square, facing in cells:
+            square = square + gz * gz
+            inverse = lax.rsqrt(square)
+            pairs.append(jnp.concatenate([here, square * inverse], axis=0))
+            shades.append(0.15 + jnp.abs(self.toward[0] * gz + facing) * inverse)
+        pair = jnp.concatenate(pairs, axis=1)
+        high = pair.astype(jnp.bfloat16)
+        low = (pair - high.astype(jnp.float32)).astype(jnp.bfloat16)
+        ones = jnp.concatenate([self.ones] * len(cells), axis=1)
+        terms = jnp.concatenate([high, low, high, low, ones], axis=0)
+        args = jnp.dot(self.mix, terms, preferred_element_type=jnp.float32)
+        args = [
+            [args[k * ROW : (k + 1) * ROW, n * LANE : (n + 1) * LANE] for k in range(CHANNELS)] for n in range(len(cells))
+        ]
+        return list(zip(shades, args))
+
+    def look_direct(self, here, gz, square, facing):
         square = square + gz * gz
         inverse = lax.rsqrt(square)
         norm = square * inverse
         shade = 0.15 + jnp.abs(self.toward[0] * gz + facing) * inverse
-        dim = jnp.exp2(self.veil[0] * here + self.veil[1] * norm + self.veil[2])
-        root = lax.rsqrt(dim + self.bound)
+        return shade, [self.rows[k][0] * here + self.rows[k][1] * norm + self.rows[k][2] for k in range(CHANNELS)]
+
+    def add(self, state, visible, shade, args):
+        alpha, plain, tinted = state
+        root = lax.rsqrt(jnp.exp2(args[3]) + self.bound)
         opacity = jnp.where(visible, root * root, 0.0)
         weight = opacity - alpha * opacity
         lit = weight * shade
-        tinted = [
-            tinted[k] + lit * jnp.tanh(self.hues[k][0] * here + self.hues[k][1] * norm + self.hues[k][2])
-            for k in range(3)
-        ]
+        tinted = [tinted[k] + lit * jnp.tanh(args[k]) for k in range(3)]
         return alpha + weight, plain + lit, tinted
 
 
@@ -144,12 +188,17 @@
         for at in range(ROW, rows - ROW, ROW):
             start = entry[at : at + ROW, cols] - origin
             state = (zero, zero, [zero] * 3)
+            cells_here = []
             before, here = bricks.load(piece, 0, at), bricks.load(piece, 1, at)
             for slab in range(1, slabs - 1):
                 after = bricks.load(piece, slab + 1, at)
                 side = bricks.lateral(shader, piece, slab, at, here)
-                state = shader.add(state, start <= slab, here, after - before, *side)
+                cells_here.append((here, after - before, *side))
                 before, here = here, after
+                if len(cells_here) == 2 or slab == slabs - 2:
+                    for n, seen_here in enumerate(shader.look(cells_here)):
+                        state = shader.add(state, start <= slab + 1 - len(cells_here) + n, *seen_here)
+                    cells_here = []
             to = pl.ds(at - ROW, ROW)
             for k in range(3):
                 seen[piece, k, to, :] = state[1] + state[2][k]
@@ -201,16 +250,15 @@
             at, src = pl.ds(row, ROW), pl.ds(row - ROW, ROW)
             start = entry[at, cols] - origin
             square, facing, inner = (ends[0, k, piece, src, :] for k in range(3))
-            alpha, plain, tinted = shader.add(
-                (zero, zero, [zero] * 3), start <= 0, near[at, cols], inner - front[at, cols], square, facing
-            )
+            first = (near[at, cols], inner - front[at, cols], square, facing)
+            square, facing, inner = (ends[1, k, piece, src, :] for k in range(3))
+            last = (far[at, cols], back[at, cols] - inner, square, facing)
+            first, last = shader.look_direct(*first), shader.look_direct(*last)
+            alpha, plain, tinted = shader.add((zero, zero, [zero] * 3), start <= 0, *first)
             clear = 1.0 - alpha
             tinted = [tinted[k] + plain + clear * seen[piece, k, src, :] for k in range(3)]
             alpha = alpha + clear * seen[piece, 3, src, :]
-            square, facing, inner = (ends[1, k, piece, src, :] for k in range(3))
-            alpha, plain, tinted = shader.add(
-                (alpha, zero, tinted), start <= slabs - 1, far[at, cols], back[at, cols] - inner, square, facing
-            )
+            alpha, plain, tinted = shader.add((alpha, zero, tinted), start <= slabs - 1, *last)
             for k in range(3):
                 out[piece, k, at, :] = plain + tinted[k]
             out[piece, 3, at, :] = alpha
@@ -234,13 +282,19 @@
         for bricks, row in ((tops, 0), (bottoms, at_last)):
             at = pl.ds(row, ROW)
             start = entry[at, cols] - origin
-            alpha, plain, tinted = zero, zero, [zero] * 3
+            state = (zero, zero, [zero] * 3)
+            cells_here = []
             before, here = front[at, cols], bricks.load(piece, 0, ROW)
             for slab in range(slabs):
                 after = back[at, cols] if slab == slabs - 1 else bricks.load(piece, slab + 1, ROW)
                 side = bricks.lateral(shader, piece, slab, ROW, here)
-                alpha, plain, tinted = shader.add((alpha, plain, tinted), start <= slab, here, after - before, *side)
+                cells_here.append((here, after - before, *side))
                 before, here = here, after
+                if len(cells_here) == 2 or slab == slabs - 1:
+                    for n, seen_here in enumerate(shader.look(cells_here)):
+                        state = shader.add(state, start <= slab + 1 - len(cells_here) + n, *seen_here)
+                    cells_here = []
+            alpha, plain, tinted = state
             for k in range(3):
                 out[piece, k, at, :] = plain + tinted[k]
             out[piece, 3, at, :] = alpha

time: 71.7 us -> 70.3 us (0.980)
  Pallas kernels: 23.3 us -> 21.9 us
    pallas_call x1, Pallas kernels: 13.5 us -> 12.3 us  [middle(): pl.pallas_call(functools.partial(middle_kernel, depth_total), in_specs=[S...]
  transfers between devices with their start and end apart: 4 -> 4, of which waited for: 0 -> 0; matrix products, arithmetic and copies ran while one was open for 0% -> 0% of each run, Pallas kernels for 19% -> 18%
where the time goes in v3:
time: 70.3 us; the launch traced here: 69.6 us
  blocking collectives  37.2 us (53%)
  Pallas kernels  21.9 us (31%)
  starting transfers between devices  10.4 us (15%)
    all_to_all x1, blocking collectives, local(): return merge(lax.all_to_all(parts, 'depth', 0, 0))  37.2 us
    pallas_call x1, Pallas kernels, middle(): pl.pallas_call(functools.partial(middle_kernel, depth_total), in_specs=[S...  12.3 us
    pallas_call x1, Pallas kernels, finish(): pl.pallas_call(functools.partial(finish_kernel, depth_total), in_specs=[S...  7.33 us
    ppermute x1, starting transfers between devices, local(): below = lax.ppermute(first_row, 'tile', [(b, a) for a, b in up_t])  3.64 us
    ppermute x1, starting transfers between devices, local(): front = lax.ppermute(last_slab, 'depth', up)  3.51 us
    ppermute x1, starting transfers between devices, local(): above = lax.ppermute(last_row, 'tile', up_t)  1.92 us
  transfers between devices with their start and end apart: 4, of which 0 were waited for; matrix products, arithmetic and copies ran while one was open for 0% of the time, Pallas kernels for 18%

profile of v3, /device:TPU:96, one launch (start us, length us, event | category | flops | bytes accessed | tf_op | source)
XLA Modules:
  0.0 69.6 jit_solution(1823019815562127465)
XLA Ops:
  0.0 0.0 copy-start.1
  0.0 0.0 copy-start.2
  0.0 0.0 copy-start
  0.0 1.4 %edges.1 = (f32[64,2048]{1,0:T(8,128)S(1)}, f32[64,2048]{1,0:T(8,128)S(1)}, f32[16,1,2048]{2,1,0:T(1,128)S(1)}, f32[16,1,2048]{2,1,0:T(1,128)S(1)}) custom-call(f32[16,64,2048]{2,1,0:T(8,128)} %volume.5), custom_call_target="tpu_custom_call" | custom-call | bytes 4194304 | tf_op jit(solution)/shard_map/edges/pallas_call | solution.py:38
  1.4 3.5 %collective-permute-start.2 = (f32[64,2048]{1,0:T(8,128)S(1)}, f32[64,2048]{1,0:T(8,128)S(1)}, u32[]{:S(2)}, u32[]{:S(2)}) collective-permute-start(f32[64,2048]{1,0:T(8,128)S(1)} %get-tuple-element.13.far), channel_id=1, source_target_pairs={{0,16},{16,32},{32,48},{48,64},{64,80},{80,96},{96,112},{112,128},... | collective-permute-start | bytes 1572872 | tf_op jit(solution)/shard_map/ppermute | solution.py:382
  4.9 1.3 %collective-permute-start.3 = (f32[64,2048]{1,0:T(8,128)S(1)}, f32[64,2048]{1,0:T(8,128)S(1)}, u32[]{:S(2)}, u32[]{:S(2)}) collective-permute-start(f32[64,2048]{1,0:T(8,128)S(1)} %get-tuple-element.14.near), channel_id=1, source_target_pairs={{16,0},{32,16},{48,32},{64,48},{80,64},{96,80},{112,96},{128,112},... | collective-permute-start | bytes 1572872 | tf_op jit(solution)/shard_map/ppermute | solution.py:383
  6.2 1.9 %collective-permute-start = (f32[16,1,2048]{2,1,0:T(1,128)S(1)}, f32[16,1,2048]{2,1,0:T(1,128)S(1)}, u32[]{:S(2)}, u32[]{:S(2)}) collective-permute-start(f32[16,1,2048]{2,1,0:T(1,128)S(1)} %get-tuple-element.11), channel_id=1, source_target_pairs={{0,1},{1,2},{2,3},{3,4},{4,5},{5,6},{6,7},{7,8},{8,9},{9,10},{10,1... | collective-permute-start | bytes 393224 | tf_op jit(solution)/shard_map/ppermute | solution.py:384
  8.1 3.6 %collective-permute-start.1 = (f32[16,1,2048]{2,1,0:T(1,128)S(1)}, f32[16,1,2048]{2,1,0:T(1,128)S(1)}, u32[]{:S(2)}, u32[]{:S(2)}) collective-permute-start(f32[16,1,2048]{2,1,0:T(1,128)S(1)} %get-tuple-element.12), channel_id=1, source_target_pairs={{1,0},{2,1},{3,2},{4,3},{5,4},{6,5},{7,6},{8,7},{9,8},{10,9},{11,1... | collective-permute-start | bytes 393224 | tf_op jit(solution)/shard_map/ppermute | solution.py:385
  11.8 0.0 copy-done.1
  11.8 0.0 copy-done.2
  11.8 0.0 copy-done
  11.8 12.3 %middle.1 = (f32[16,4,48,128]{3,2,1,0:T(8,128)S(1)}, f32[2,3,16,48,128]{4,3,2,1,0:T(8,128)S(1)}) custom-call(f32[3]{0:T(128)S(1)} %copy-done.2, f32[4,3]{1,0:T(4,128)S(1)} %copy-done.1, s32[1]{0:T(128)} %bitcast.base, f32[16,64,2048]{2,1,0:T(8,128)} %volume.5, s32[64,2048]{1,0:T(8,128)S(1)} %copy-done), custom_call_target="tpu_custom_call" | custom-call | flops 82575360 | bytes 5505024 | tf_op jit(solution)/shard_map/middle/pallas_call | solution.py:310
  24.2 0.0 collective-permute-done.above
  24.2 0.0 collective-permute-done.1.below
  24.2 0.0 collective-permute-done.2.front
  24.2 0.0 collective-permute-done.3.back
  24.2 7.3 %finish.1 = f32[16,4,64,128]{3,2,1,0:T(8,128)S(1)} custom-call(f32[3]{0:T(128)S(1)} %copy-done.2, f32[4,3]{1,0:T(4,128)S(1)} %copy-done.1, s32[1]{0:T(128)} %bitcast.base, f32[16,64,2048]{2,1,0:T(8,128)} %volume.5, s32[64,2048]{1,0:T(8,128)S(1)} %copy-done, f32[16,1,2048]{2,1,0:T(1,128)S(1)} %collective-permute-done.above, ...), custom_call_target="tpu_custom_call" | custom-call | flops 47185920 | bytes 3145728 | tf_op jit(solution)/shard_map/finish/pallas_call | solution.py:333
  31.5 37.2 %all_to_all.5.parts = f32[16,4,64,128]{3,2,1,0:T(8,128)S(1)} all-to-all(f32[16,4,64,128]{3,2,1,0:T(8,128)S(1)} %finish.1), channel_id=1, replica_groups=mesh['depth'=16,'tile'=16] {'depth'}, dimensions={0} | all-to-all | bytes 4194304 | tf_op jit(solution)/shard_map/all_to_all | solution.py:392
  68.8 0.9 %merge.1 = f32[4,64,128]{2,1,0:T(8,128)} custom-call(f32[16,4,64,128]{3,2,1,0:T(8,128)S(1)} %all_to_all.5.parts), custom_call_target="tpu_custom_call" | custom-call | flops 524288 | bytes 2097152 | tf_op jit(solution)/shard_map/merge/pallas_call | solution.py:364
Async XLA Ops:
  0.0 11.8 %copy-start.1 = (f32[4,3]{1,0:T(4,128)S(1)}, f32[4,3]{1,0:T(4,128)}, u32[]{:S(2)}) copy-start(f32[4,3]{1,0:T(4,128)} %transfer.3) | copy-start | bytes 148
  0.0 11.8 %copy-start.2 = (f32[3]{0:T(128)S(1)}, f32[3]{0:T(128)}, u32[]{:S(2)}) copy-start(f32[3]{0:T(128)} %light.3) | copy-start | bytes 40
  0.0 11.8 %copy-start = (s32[64,2048]{1,0:T(8,128)S(1)}, s32[64,2048]{1,0:T(8,128)}, u32[]{:S(2)}) copy-start(s32[64,2048]{1,0:T(8,128)} %entry.3) | copy-start | bytes 1572868
  1.4 22.8 %collective-permute-start.2 = (f32[64,2048]{1,0:T(8,128)S(1)}, f32[64,2048]{1,0:T(8,128)S(1)}, u32[]{:S(2)}, u32[]{:S(2)}) collective-permute-start(f32[64,2048]{1,0:T(8,128)S(1)} %get-tuple-element.13.far), channel_id=1, source_target_pairs={{0,16},{16,32},{32,48},{48,64},{64,80},{80,96},{96,112},{112,128},... | collective-permute-start | bytes 1572872 | tf_op jit(solution)/shard_map/ppermute | solution.py:382
  4.9 19.3 %collective-permute-start.3 = (f32[64,2048]{1,0:T(8,128)S(1)}, f32[64,2048]{1,0:T(8,128)S(1)}, u32[]{:S(2)}, u32[]{:S(2)}) collective-permute-start(f32[64,2048]{1,0:T(8,128)S(1)} %get-tuple-element.14.near), channel_id=1, source_target_pairs={{16,0},{32,16},{48,32},{64,48},{80,64},{96,80},{112,96},{128,112},... | collective-permute-start | bytes 1572872 | tf_op jit(solution)/shard_map/ppermute | solution.py:383
  6.2 18.0 %collective-permute-start = (f32[16,1,2048]{2,1,0:T(1,128)S(1)}, f32[16,1,2048]{2,1,0:T(1,128)S(1)}, u32[]{:S(2)}, u32[]{:S(2)}) collective-permute-start(f32[16,1,2048]{2,1,0:T(1,128)S(1)} %get-tuple-element.11), channel_id=1, source_target_pairs={{0,1},{1,2},{2,3},{3,4},{4,5},{5,6},{6,7},{7,8},{8,9},{9,10},{10,1... | collective-permute-start | bytes 393224 | tf_op jit(solution)/shard_map/ppermute | solution.py:384
  8.1 16.0 %collective-permute-start.1 = (f32[16,1,2048]{2,1,0:T(1,128)S(1)}, f32[16,1,2048]{2,1,0:T(1,128)S(1)}, u32[]{:S(2)}, u32[]{:S(2)}) collective-permute-start(f32[16,1,2048]{2,1,0:T(1,128)S(1)} %get-tuple-element.12), channel_id=1, source_target_pairs={{1,0},{2,1},{3,2},{4,3},{5,4},{6,5},{7,6},{8,7},{9,8},{10,9},{11,1... | collective-permute-start | bytes 393224 | tf_op jit(solution)/shard_map/ppermute | solution.py:385

commit v4 on v3

--- a/solution.py
+++ b/solution.py
@@ -12,6 +12,7 @@
 LANE = 128
 LOG2E = 1.4426950408889634
 CHANNELS = 4
+GROUP = 2
 VMEM = pl.BlockSpec(memory_space=pltpu.VMEM)
 SMEM = pl.BlockSpec(memory_space=pltpu.SMEM)
 HBM = pl.BlockSpec(memory_space=pl.ANY)
@@ -179,37 +180,42 @@
     zero = jnp.zeros((ROW, LANE), jnp.float32)
     fetch(0).wait()
 
-    def column(piece, carry):
-        @pl.when(piece < pieces - 1)
+    def columns_of(group, carry):
+        for member in range(1, GROUP):
+            fetch(group * GROUP + member).wait()
+
+        @pl.when(group < pieces // GROUP - 1)
         def _():
-            fetch(piece + 1).wait()
-
-        cols = pl.ds(pl.multiple_of(piece * LANE, LANE), LANE)
-        for at in range(ROW, rows - ROW, ROW):
-            start = entry[at : at + ROW, cols] - origin
-            state = (zero, zero, [zero] * 3)
-            cells_here = []
-            before, here = bricks.load(piece, 0, at), bricks.load(piece, 1, at)
-            for slab in range(1, slabs - 1):
-                after = bricks.load(piece, slab + 1, at)
-                side = bricks.lateral(shader, piece, slab, at, here)
-                cells_here.append((here, after - before, *side))
-                before, here = here, after
-                if len(cells_here) == 2 or slab == slabs - 2:
-                    for n, seen_here in enumerate(shader.look(cells_here)):
-                        state = shader.add(state, start <= slab + 1 - len(cells_here) + n, *seen_here)
-                    cells_here = []
-            to = pl.ds(at - ROW, ROW)
-            for k in range(3):
-                seen[piece, k, to, :] = state[1] + state[2][k]
-            seen[piece, 3, to, :] = state[0]
-            for end, (slab, inner) in enumerate(((0, 1), (slabs - 1, slabs - 2))):
-                side = bricks.lateral(shader, piece, slab, at, bricks.load(piece, slab, at))
-                for k, value in enumerate((*side, bricks.load(piece, inner, at))):
-                    ends[end, k, piece, to, :] = value
-        return carry
-
-    lax.fori_loop(0, pieces, column, 0)
+            fetch(group * GROUP + GROUP).wait()
+
+        for member in range(GROUP):
+            piece = group * GROUP + member
+            cols = pl.ds(pl.multiple_of(piece * LANE, LANE), LANE)
+            for at in range(ROW, rows - ROW, ROW):
+                start = entry[at : at + ROW, cols] - origin
+                state = (zero, zero, [zero] * 3)
+                cells_here = []
+                before, here = bricks.load(piece, 0, at), bricks.load(piece, 1, at)
+                for slab in range(1, slabs - 1):
+                    after = bricks.load(piece, slab + 1, at)
+                    side = bricks.lateral(shader, piece, slab, at, here)
+                    cells_here.append((here, after - before, *side))
+                    before, here = here, after
+                    if len(cells_here) == 2 or slab == slabs - 2:
+                        for n, seen_here in enumerate(shader.look(cells_here)):
+                            state = shader.add(state, start <= slab + 1 - len(cells_here) + n, *seen_here)
+                        cells_here = []
+                to = pl.ds(at - ROW, ROW)
+                for k in range(3):
+                    seen[piece, k, to, :] = state[1] + state[2][k]
+                seen[piece, 3, to, :] = state[0]
+                for end, (slab, inner) in enumerate(((0, 1), (slabs - 1, slabs - 2))):
+                    side = bricks.lateral(shader, piece, slab, at, bricks.load(piece, slab, at))
+                    for k, value in enumerate((*side, bricks.load(piece, inner, at))):
+                        ends[end, k, piece, to, :] = value
+        return carry
+
+    lax.fori_loop(0, pieces // GROUP, columns_of, 0)
 
 
 def finish_kernel(
@@ -300,7 +306,7 @@
             out[piece, 3, at, :] = alpha
         return carry
 
-    lax.fori_loop(0, pieces, rims, 0, unroll=2)
+    lax.fori_loop(0, pieces, rims, 0, unroll=8)
 
 
 def middle(volume, entry, light, transfer, base, depth_total):

time: 70.3 us -> 69 us (0.982)
  Pallas kernels: 21.9 us -> 20.6 us
  transfers between devices with their start and end apart: 4 -> 4, of which waited for: 0 -> 0; matrix products, arithmetic and copies ran while one was open for 0% -> 0% of each run, Pallas kernels for 18% -> 17%
where the time goes in v4:
time: 69 us; the launch traced here: 68.3 us
  blocking collectives  37.2 us (54%)
  Pallas kernels  20.6 us (30%)
  starting transfers between devices  10.4 us (15%)
    all_to_all x1, blocking collectives, local(): return merge(lax.all_to_all(parts, 'depth', 0, 0))  37.2 us
    pallas_call x1, Pallas kernels, middle(): pl.pallas_call(functools.partial(middle_kernel, depth_total), in_specs=[S...  11.7 us
    pallas_call x1, Pallas kernels, finish(): pl.pallas_call(functools.partial(finish_kernel, depth_total), in_specs=[S...  6.69 us
    ppermute x1, starting transfers between devices, local(): below = lax.ppermute(first_row, 'tile', [(b, a) for a, b in up_t])  3.64 us
    ppermute x1, starting transfers between devices, local(): front = lax.ppermute(last_slab, 'depth', up)  3.51 us
    ppermute x1, starting transfers between devices, local(): above = lax.ppermute(last_row, 'tile', up_t)  1.92 us
  transfers between devices with their start and end apart: 4, of which 0 were waited for; matrix products, arithmetic and copies ran while one was open for 0% of the time, Pallas kernels for 17%

profile of v4, /device:TPU:96, one launch (start us, length us, event | category | flops | bytes accessed | tf_op | source)
XLA Modules:
  0.0 68.3 jit_solution(16371758497476047890)
XLA Ops:
  0.0 0.0 copy-start.1
  0.0 0.0 copy-start.2
  0.0 0.0 copy-start
  0.0 1.4 %edges.1 = (f32[64,2048]{1,0:T(8,128)S(1)}, f32[64,2048]{1,0:T(8,128)S(1)}, f32[16,1,2048]{2,1,0:T(1,128)S(1)}, f32[16,1,2048]{2,1,0:T(1,128)S(1)}) custom-call(f32[16,64,2048]{2,1,0:T(8,128)} %volume.5), custom_call_target="tpu_custom_call" | custom-call | bytes 4194304 | tf_op jit(solution)/shard_map/edges/pallas_call | solution.py:39
  1.4 3.5 %collective-permute-start.2 = (f32[64,2048]{1,0:T(8,128)S(1)}, f32[64,2048]{1,0:T(8,128)S(1)}, u32[]{:S(2)}, u32[]{:S(2)}) collective-permute-start(f32[64,2048]{1,0:T(8,128)S(1)} %get-tuple-element.13.far), channel_id=1, source_target_pairs={{0,16},{16,32},{32,48},{48,64},{64,80},{80,96},{96,112},{112,128},... | collective-permute-start | bytes 1572872 | tf_op jit(solution)/shard_map/ppermute | solution.py:388
  4.9 1.3 %collective-permute-start.3 = (f32[64,2048]{1,0:T(8,128)S(1)}, f32[64,2048]{1,0:T(8,128)S(1)}, u32[]{:S(2)}, u32[]{:S(2)}) collective-permute-start(f32[64,2048]{1,0:T(8,128)S(1)} %get-tuple-element.14.near), channel_id=1, source_target_pairs={{16,0},{32,16},{48,32},{64,48},{80,64},{96,80},{112,96},{128,112},... | collective-permute-start | bytes 1572872 | tf_op jit(solution)/shard_map/ppermute | solution.py:389
  6.2 1.9 %collective-permute-start = (f32[16,1,2048]{2,1,0:T(1,128)S(1)}, f32[16,1,2048]{2,1,0:T(1,128)S(1)}, u32[]{:S(2)}, u32[]{:S(2)}) collective-permute-start(f32[16,1,2048]{2,1,0:T(1,128)S(1)} %get-tuple-element.11), channel_id=1, source_target_pairs={{0,1},{1,2},{2,3},{3,4},{4,5},{5,6},{6,7},{7,8},{8,9},{9,10},{10,1... | collective-permute-start | bytes 393224 | tf_op jit(solution)/shard_map/ppermute | solution.py:390
  8.1 3.6 %collective-permute-start.1 = (f32[16,1,2048]{2,1,0:T(1,128)S(1)}, f32[16,1,2048]{2,1,0:T(1,128)S(1)}, u32[]{:S(2)}, u32[]{:S(2)}) collective-permute-start(f32[16,1,2048]{2,1,0:T(1,128)S(1)} %get-tuple-element.12), channel_id=1, source_target_pairs={{1,0},{2,1},{3,2},{4,3},{5,4},{6,5},{7,6},{8,7},{9,8},{10,9},{11,1... | collective-permute-start | bytes 393224 | tf_op jit(solution)/shard_map/ppermute | solution.py:391
  11.8 0.0 copy-done.1
  11.8 0.0 copy-done.2
  11.8 0.0 copy-done
  11.8 11.7 %middle.1 = (f32[16,4,48,128]{3,2,1,0:T(8,128)S(1)}, f32[2,3,16,48,128]{4,3,2,1,0:T(8,128)S(1)}) custom-call(f32[3]{0:T(128)S(1)} %copy-done.2, f32[4,3]{1,0:T(4,128)S(1)} %copy-done.1, s32[1]{0:T(128)} %bitcast.base, f32[16,64,2048]{2,1,0:T(8,128)} %volume.5, s32[64,2048]{1,0:T(8,128)S(1)} %copy-done), custom_call_target="tpu_custom_call" | custom-call | flops 82575360 | bytes 5505024 | tf_op jit(solution)/shard_map/middle/pallas_call | solution.py:316
  23.5 0.0 collective-permute-done.above
  23.5 0.0 collective-permute-done.1.below
  23.5 0.0 collective-permute-done.2.front
  23.5 0.0 collective-permute-done.3.back
  23.5 6.7 %finish.1 = f32[16,4,64,128]{3,2,1,0:T(8,128)S(1)} custom-call(f32[3]{0:T(128)S(1)} %copy-done.2, f32[4,3]{1,0:T(4,128)S(1)} %copy-done.1, s32[1]{0:T(128)} %bitcast.base, f32[16,64,2048]{2,1,0:T(8,128)} %volume.5, s32[64,2048]{1,0:T(8,128)S(1)} %copy-done, f32[16,1,2048]{2,1,0:T(1,128)S(1)} %collective-permute-done.above, ...), custom_call_target="tpu_custom_call" | custom-call | flops 47185920 | bytes 3145728 | tf_op jit(solution)/shard_map/finish/pallas_call | solution.py:339
  30.2 37.2 %all_to_all.5.parts = f32[16,4,64,128]{3,2,1,0:T(8,128)S(1)} all-to-all(f32[16,4,64,128]{3,2,1,0:T(8,128)S(1)} %finish.1), channel_id=1, replica_groups=mesh['depth'=16,'tile'=16] {'depth'}, dimensions={0} | all-to-all | bytes 4194304 | tf_op jit(solution)/shard_map/all_to_all | solution.py:398
  67.5 0.9 %merge.1 = f32[4,64,128]{2,1,0:T(8,128)} custom-call(f32[16,4,64,128]{3,2,1,0:T(8,128)S(1)} %all_to_all.5.parts), custom_call_target="tpu_custom_call" | custom-call | flops 524288 | bytes 2097152 | tf_op jit(solution)/shard_map/merge/pallas_call | solution.py:370
Async XLA Ops:
  0.0 11.8 %copy-start.1 = (f32[4,3]{1,0:T(4,128)S(1)}, f32[4,3]{1,0:T(4,128)}, u32[]{:S(2)}) copy-start(f32[4,3]{1,0:T(4,128)} %transfer.3) | copy-start | bytes 148
  0.0 11.8 %copy-start.2 = (f32[3]{0:T(128)S(1)}, f32[3]{0:T(128)}, u32[]{:S(2)}) copy-start(f32[3]{0:T(128)} %light.3) | copy-start | bytes 40
  0.0 11.8 %copy-start = (s32[64,2048]{1,0:T(8,128)S(1)}, s32[64,2048]{1,0:T(8,128)}, u32[]{:S(2)}) copy-start(s32[64,2048]{1,0:T(8,128)} %entry.3) | copy-start | bytes 1572868
  1.4 22.2 %collective-permute-start.2 = (f32[64,2048]{1,0:T(8,128)S(1)}, f32[64,2048]{1,0:T(8,128)S(1)}, u32[]{:S(2)}, u32[]{:S(2)}) collective-permute-start(f32[64,2048]{1,0:T(8,128)S(1)} %get-tuple-element.13.far), channel_id=1, source_target_pairs={{0,16},{16,32},{32,48},{48,64},{64,80},{80,96},{96,112},{112,128},... | collective-permute-start | bytes 1572872 | tf_op jit(solution)/shard_map/ppermute | solution.py:388
  4.9 18.6 %collective-permute-start.3 = (f32[64,2048]{1,0:T(8,128)S(1)}, f32[64,2048]{1,0:T(8,128)S(1)}, u32[]{:S(2)}, u32[]{:S(2)}) collective-permute-start(f32[64,2048]{1,0:T(8,128)S(1)} %get-tuple-element.14.near), channel_id=1, source_target_pairs={{16,0},{32,16},{48,32},{64,48},{80,64},{96,80},{112,96},{128,112},... | collective-permute-start | bytes 1572872 | tf_op jit(solution)/shard_map/ppermute | solution.py:389
  6.2 17.3 %collective-permute-start = (f32[16,1,2048]{2,1,0:T(1,128)S(1)}, f32[16,1,2048]{2,1,0:T(1,128)S(1)}, u32[]{:S(2)}, u32[]{:S(2)}) collective-permute-start(f32[16,1,2048]{2,1,0:T(1,128)S(1)} %get-tuple-element.11), channel_id=1, source_target_pairs={{0,1},{1,2},{2,3},{3,4},{4,5},{5,6},{6,7},{7,8},{8,9},{9,10},{10,1... | collective-permute-start | bytes 393224 | tf_op jit(solution)/shard_map/ppermute | solution.py:390
  8.1 15.4 %collective-permute-start.1 = (f32[16,1,2048]{2,1,0:T(1,128)S(1)}, f32[16,1,2048]{2,1,0:T(1,128)S(1)}, u32[]{:S(2)}, u32[]{:S(2)}) collective-permute-start(f32[16,1,2048]{2,1,0:T(1,128)S(1)} %get-tuple-element.12), channel_id=1, source_target_pairs={{1,0},{2,1},{3,2},{4,3},{5,4},{6,5},{7,6},{8,7},{9,8},{10,9},{11,1... | collective-permute-start | bytes 393224 | tf_op jit(solution)/shard_map/ppermute | solution.py:391

commit v5 on v4

--- a/solution.py
+++ b/solution.py
@@ -270,7 +270,7 @@
             out[piece, 3, at, :] = alpha
         return carry
 
-    lax.fori_loop(0, pieces, closing, 0)
+    lax.fori_loop(0, pieces, closing, 0, unroll=4)
 
     def ready(piece, carry):
         for copy in fetches(piece):
@@ -281,7 +281,7 @@
             lower[piece + 1, slab, 2 * ROW : 2 * ROW + 1, :] = below[slab, :, cols]
         return carry
 
-    lax.fori_loop(0, pieces, ready, 0)
+    lax.fori_loop(0, pieces, ready, 0, unroll=4)
 
     def rims(piece, carry):
         cols = pl.ds(pl.multiple_of(piece * LANE, LANE), LANE)
@@ -306,7 +306,7 @@
             out[piece, 3, at, :] = alpha
         return carry
 
-    lax.fori_loop(0, pieces, rims, 0, unroll=8)
+    lax.fori_loop(0, pieces, rims, 0, unroll=16)
 
 
 def middle(volume, entry, light, transfer, base, depth_total):
@@ -362,7 +362,7 @@
             out[k, at, :] = total[k]
         return carry
 
-    lax.fori_loop(0, rows // ROW, rows_of, 0, unroll=2)
+    lax.fori_loop(0, rows // ROW, rows_of, 0, unroll=8)
 
 
 def merge(parts):

time: 69 us -> 68.8 us (level)
  no operation moved by 1% of the time
where the time goes in v5:
time: 68.8 us; the launch traced here: 68.2 us
  blocking collectives  37.2 us (54%)
  Pallas kernels  20.4 us (30%)
  starting transfers between devices  10.4 us (15%)
    all_to_all x1, blocking collectives, local(): return merge(lax.all_to_all(parts, 'depth', 0, 0))  37.2 us
    pallas_call x1, Pallas kernels, middle(): pl.pallas_call(functools.partial(middle_kernel, depth_total), in_specs=[S...  11.7 us
    pallas_call x1, Pallas kernels, finish(): pl.pallas_call(functools.partial(finish_kernel, depth_total), in_specs=[S...  6.58 us
    ppermute x1, starting transfers between devices, local(): below = lax.ppermute(first_row, 'tile', [(b, a) for a, b in up_t])  3.64 us
    ppermute x1, starting transfers between devices, local(): front = lax.ppermute(last_slab, 'depth', up)  3.51 us
    ppermute x1, starting transfers between devices, local(): above = lax.ppermute(last_row, 'tile', up_t)  1.92 us
  transfers between devices with their start and end apart: 4, of which 0 were waited for; matrix products, arithmetic and copies ran while one was open for 0% of the time, Pallas kernels for 17%

profile of v5, /device:TPU:96, one launch (start us, length us, event | category | flops | bytes accessed | tf_op | source)
XLA Modules:
  0.0 68.2 jit_solution(11436248693286304605)
XLA Ops:
  0.0 0.0 copy-start.1
  0.0 0.0 copy-start.2
  0.0 0.0 copy-start
  0.0 1.4 %edges.1 = (f32[64,2048]{1,0:T(8,128)S(1)}, f32[64,2048]{1,0:T(8,128)S(1)}, f32[16,1,2048]{2,1,0:T(1,128)S(1)}, f32[16,1,2048]{2,1,0:T(1,128)S(1)}) custom-call(f32[16,64,2048]{2,1,0:T(8,128)} %volume.5), custom_call_target="tpu_custom_call" | custom-call | bytes 4194304 | tf_op jit(solution)/shard_map/edges/pallas_call | solution.py:39
  1.4 3.5 %collective-permute-start.2 = (f32[64,2048]{1,0:T(8,128)S(1)}, f32[64,2048]{1,0:T(8,128)S(1)}, u32[]{:S(2)}, u32[]{:S(2)}) collective-permute-start(f32[64,2048]{1,0:T(8,128)S(1)} %get-tuple-element.13.far), channel_id=1, source_target_pairs={{0,16},{16,32},{32,48},{48,64},{64,80},{80,96},{96,112},{112,128},... | collective-permute-start | bytes 1572872 | tf_op jit(solution)/shard_map/ppermute | solution.py:388
  4.9 1.3 %collective-permute-start.3 = (f32[64,2048]{1,0:T(8,128)S(1)}, f32[64,2048]{1,0:T(8,128)S(1)}, u32[]{:S(2)}, u32[]{:S(2)}) collective-permute-start(f32[64,2048]{1,0:T(8,128)S(1)} %get-tuple-element.14.near), channel_id=1, source_target_pairs={{16,0},{32,16},{48,32},{64,48},{80,64},{96,80},{112,96},{128,112},... | collective-permute-start | bytes 1572872 | tf_op jit(solution)/shard_map/ppermute | solution.py:389
  6.2 1.9 %collective-permute-start = (f32[16,1,2048]{2,1,0:T(1,128)S(1)}, f32[16,1,2048]{2,1,0:T(1,128)S(1)}, u32[]{:S(2)}, u32[]{:S(2)}) collective-permute-start(f32[16,1,2048]{2,1,0:T(1,128)S(1)} %get-tuple-element.11), channel_id=1, source_target_pairs={{0,1},{1,2},{2,3},{3,4},{4,5},{5,6},{6,7},{7,8},{8,9},{9,10},{10,1... | collective-permute-start | bytes 393224 | tf_op jit(solution)/shard_map/ppermute | solution.py:390
  8.1 3.6 %collective-permute-start.1 = (f32[16,1,2048]{2,1,0:T(1,128)S(1)}, f32[16,1,2048]{2,1,0:T(1,128)S(1)}, u32[]{:S(2)}, u32[]{:S(2)}) collective-permute-start(f32[16,1,2048]{2,1,0:T(1,128)S(1)} %get-tuple-element.12), channel_id=1, source_target_pairs={{1,0},{2,1},{3,2},{4,3},{5,4},{6,5},{7,6},{8,7},{9,8},{10,9},{11,1... | collective-permute-start | bytes 393224 | tf_op jit(solution)/shard_map/ppermute | solution.py:391
  11.8 0.0 copy-done.1
  11.8 0.0 copy-done.2
  11.8 0.0 copy-done
  11.8 11.7 %middle.1 = (f32[16,4,48,128]{3,2,1,0:T(8,128)S(1)}, f32[2,3,16,48,128]{4,3,2,1,0:T(8,128)S(1)}) custom-call(f32[3]{0:T(128)S(1)} %copy-done.2, f32[4,3]{1,0:T(4,128)S(1)} %copy-done.1, s32[1]{0:T(128)} %bitcast.base, f32[16,64,2048]{2,1,0:T(8,128)} %volume.5, s32[64,2048]{1,0:T(8,128)S(1)} %copy-done), custom_call_target="tpu_custom_call" | custom-call | flops 82575360 | bytes 5505024 | tf_op jit(solution)/shard_map/middle/pallas_call | solution.py:316
  23.5 0.0 collective-permute-done.above
  23.5 0.0 collective-permute-done.1.below
  23.5 0.0 collective-permute-done.2.front
  23.5 0.0 collective-permute-done.3.back
  23.5 6.6 %finish.1 = f32[16,4,64,128]{3,2,1,0:T(8,128)S(1)} custom-call(f32[3]{0:T(128)S(1)} %copy-done.2, f32[4,3]{1,0:T(4,128)S(1)} %copy-done.1, s32[1]{0:T(128)} %bitcast.base, f32[16,64,2048]{2,1,0:T(8,128)} %volume.5, s32[64,2048]{1,0:T(8,128)S(1)} %copy-done, f32[16,1,2048]{2,1,0:T(1,128)S(1)} %collective-permute-done.above, ...), custom_call_target="tpu_custom_call" | custom-call | flops 47185920 | bytes 3145728 | tf_op jit(solution)/shard_map/finish/pallas_call | solution.py:339
  30.1 37.2 %all_to_all.5.parts = f32[16,4,64,128]{3,2,1,0:T(8,128)S(1)} all-to-all(f32[16,4,64,128]{3,2,1,0:T(8,128)S(1)} %finish.1), channel_id=1, replica_groups=mesh['depth'=16,'tile'=16] {'depth'}, dimensions={0} | all-to-all | bytes 4194304 | tf_op jit(solution)/shard_map/all_to_all | solution.py:398
  67.4 0.8 %merge.1 = f32[4,64,128]{2,1,0:T(8,128)} custom-call(f32[16,4,64,128]{3,2,1,0:T(8,128)S(1)} %all_to_all.5.parts), custom_call_target="tpu_custom_call" | custom-call | flops 524288 | bytes 2097152 | tf_op jit(solution)/shard_map/merge/pallas_call | solution.py:370
Async XLA Ops:
  0.0 11.8 %copy-start.1 = (f32[4,3]{1,0:T(4,128)S(1)}, f32[4,3]{1,0:T(4,128)}, u32[]{:S(2)}) copy-start(f32[4,3]{1,0:T(4,128)} %transfer.3) | copy-start | bytes 148
  0.0 11.8 %copy-start.2 = (f32[3]{0:T(128)S(1)}, f32[3]{0:T(128)}, u32[]{:S(2)}) copy-start(f32[3]{0:T(128)} %light.3) | copy-start | bytes 40
  0.0 11.8 %copy-start = (s32[64,2048]{1,0:T(8,128)S(1)}, s32[64,2048]{1,0:T(8,128)}, u32[]{:S(2)}) copy-start(s32[64,2048]{1,0:T(8,128)} %entry.3) | copy-start | bytes 1572868
  1.4 22.2 %collective-permute-start.2 = (f32[64,2048]{1,0:T(8,128)S(1)}, f32[64,2048]{1,0:T(8,128)S(1)}, u32[]{:S(2)}, u32[]{:S(2)}) collective-permute-start(f32[64,2048]{1,0:T(8,128)S(1)} %get-tuple-element.13.far), channel_id=1, source_target_pairs={{0,16},{16,32},{32,48},{48,64},{64,80},{80,96},{96,112},{112,128},... | collective-permute-start | bytes 1572872 | tf_op jit(solution)/shard_map/ppermute | solution.py:388
  4.9 18.6 %collective-permute-start.3 = (f32[64,2048]{1,0:T(8,128)S(1)}, f32[64,2048]{1,0:T(8,128)S(1)}, u32[]{:S(2)}, u32[]{:S(2)}) collective-permute-start(f32[64,2048]{1,0:T(8,128)S(1)} %get-tuple-element.14.near), channel_id=1, source_target_pairs={{16,0},{32,16},{48,32},{64,48},{80,64},{96,80},{112,96},{128,112},... | collective-permute-start | bytes 1572872 | tf_op jit(solution)/shard_map/ppermute | solution.py:389
  6.2 17.3 %collective-permute-start = (f32[16,1,2048]{2,1,0:T(1,128)S(1)}, f32[16,1,2048]{2,1,0:T(1,128)S(1)}, u32[]{:S(2)}, u32[]{:S(2)}) collective-permute-start(f32[16,1,2048]{2,1,0:T(1,128)S(1)} %get-tuple-element.11), channel_id=1, source_target_pairs={{0,1},{1,2},{2,3},{3,4},{4,5},{5,6},{6,7},{7,8},{8,9},{9,10},{10,1... | collective-permute-start | bytes 393224 | tf_op jit(solution)/shard_map/ppermute | solution.py:390
  8.1 15.4 %collective-permute-start.1 = (f32[16,1,2048]{2,1,0:T(1,128)S(1)}, f32[16,1,2048]{2,1,0:T(1,128)S(1)}, u32[]{:S(2)}, u32[]{:S(2)}) collective-permute-start(f32[16,1,2048]{2,1,0:T(1,128)S(1)} %get-tuple-element.12), channel_id=1, source_target_pairs={{1,0},{2,1},{3,2},{4,3},{5,4},{6,5},{7,6},{8,7},{9,8},{10,9},{11,1... | collective-permute-start | bytes 393224 | tf_op jit(solution)/shard_map/ppermute | solution.py:391
